TPU v7x, 32 devices: a whole 2x2x4 slice. The times are simulated.
32 devices in a mesh: head: 4 (over x, core), ctx: 8 (over z, y).
Axes of the slice: x: 2, y: 2, z: 4, core: 2. Of those that a mesh axis runs over, the one named last changes fastest.
Arguments:
- query: bfloat16 [8, 512, 512], P('ctx', 'head'), may hold values from -36 to 36
- key: bfloat16 [8, 512, 512], P('ctx', 'head'), may hold values from -36 to 36
- value: bfloat16 [8, 512, 512], P('ctx', 'head'), may hold values from -6 to 6
- resid_in: bfloat16 [8, 512, 1024], P('ctx', 'head'), may hold values from -6 to 6
- out_grad: bfloat16 [8, 512, 1024], P('ctx', 'head'), may hold values from -6 to 6
- out_weight: bfloat16 [512, 1024], replicated, may hold values from -0.25 to 0.25
- conv_kernel: bfloat16 [31, 1024], replicated, may hold values from -1 to 1
- frame_lengths: int32 [8], replicated, may hold values from 256 to 512, as said below
Outputs:
- d_resid: bfloat16 [8, 512, 1024], P('ctx', None, 'head')
- d_query: bfloat16 [8, 512, 512], P('ctx', None, 'head')
- d_key: bfloat16 [8, 512, 512], P('ctx', None, 'head')
- d_value: bfloat16 [8, 512, 512], P('ctx', None, 'head')
Inputs may be any that keep to these rules, and one draw needn't show every extreme that they name: Block b holds audio in its first frame_lengths[b] frames; at least one block is full.
All inputs are finite; a program needn't handle non-finite values.
Results may differ from a plain program's by a relative error of at most 0.0086.
Values may be sent and summed in bfloat16 or wider, within the bound.
No kernel may reach another device: no remote copies, remote signals or barrier semaphores. Data moves between devices by JAX's collectives and lax.ppermute only.
A program may use at most 128 MiB of HBM per device.

v0:
```python
import jax
import jax.numpy as jnp
from jax import lax
from jax.sharding import PartitionSpec as P

HEAD_DIM = 64
KERNEL = 31
REACH = 2


def padded(cells, sides, width):
    for axis, dim in sides:
        count = lax.axis_size(axis)
        ends = count - 1
        head = lax.slice_in_dim(cells, 0, width, axis=dim)
        tail = lax.slice_in_dim(cells, cells.shape[dim] - width, cells.shape[dim], axis=dim)
        cells = jnp.concatenate(
            [
                lax.ppermute(tail, axis, [(i, (i + 1) % count) for i in range(ends)]),
                cells,
                lax.ppermute(head, axis, [((i + 1) % count, i) for i in range(ends)]),
            ],
            axis=dim,
        )
    return cells


def shifted(value, axis, steps):
    count = lax.axis_size(axis)
    first, last = (max(0, -steps), min(count, count - steps))
    return lax.ppermute(value, axis, [(source, source + steps) for source in range(first, last)])


def swish_slope(before):
    logistic = jax.nn.sigmoid(before)
    return logistic * (1.0 + before * (1.0 - logistic))


def conv_backward(resid_wide, grad_wide, weights_here, frames_here):
    margin = (KERNEL - 1) // 2
    channels = resid_wide.shape[1]
    extent = frames_here + 2 * margin
    conv_pre = jnp.zeros((extent, channels), jnp.float32)
    for offset in range(KERNEL):
        conv_pre = conv_pre + weights_here[offset] * resid_wide[offset : offset + extent]
    conv_grad = grad_wide[margin : margin + extent] * swish_slope(conv_pre)
    total = grad_wide[2 * margin : 2 * margin + frames_here]
    for offset in range(KERNEL):
        start_at = 2 * margin - offset
        total = total + weights_here[offset] * conv_grad[start_at : start_at + frames_here]
    return total.astype(jnp.bfloat16)


def on_device(query, key, value, resid_in, out_grad, out_weight, conv_kernel, frame_lengths):
    margin = (KERNEL - 1) // 2
    reach_rows = 2 * margin
    head_place = lax.axis_index("head")
    moved = (
        lax.all_to_all(query, "head", split_axis=2, concat_axis=1, tiled=True),
        lax.all_to_all(key, "head", split_axis=2, concat_axis=1, tiled=True),
        lax.all_to_all(value, "head", split_axis=2, concat_axis=1, tiled=True),
        lax.all_to_all(resid_in, "head", split_axis=2, concat_axis=1, tiled=True),
        lax.all_to_all(out_grad, "head", split_axis=2, concat_axis=1, tiled=True),
    )
    query_rows = moved[0][0]
    key_rows = moved[1][0]
    value_rows = moved[2][0]
    resid_rows = moved[3][0]
    grad_rows = moved[4][0]
    block_frames = resid_rows.shape[0]
    channels = resid_rows.shape[1]
    weights_here = lax.dynamic_slice_in_dim(conv_kernel, head_place * channels, channels, 1).astype(
        jnp.float32
    )
    resid_ext, grad_ext = (
        padded(resid_rows, (("ctx", 0),), reach_rows),
        padded(grad_rows, (("ctx", 0),), reach_rows),
    )
    d_resid = conv_backward(
        resid_ext.astype(jnp.float32), grad_ext.astype(jnp.float32), weights_here, block_frames
    )
    width_cols = query_rows.shape[1]
    weight_rows = lax.dynamic_slice_in_dim(out_weight, head_place * width_cols, width_cols, 0)
    head_sum = lax.dot_general(
        lax.all_gather(d_resid, "head", axis=1, tiled=True),
        weight_rows,
        (((1,), (1,)), ((), ())),
        preferred_element_type=jnp.float32,
    )
    head_grad = head_sum.astype(jnp.bfloat16)
    d_resid_out = d_resid[None]
    frames_here = query_rows.shape[0]
    width_here = query_rows.shape[1]
    heads_here = width_here // HEAD_DIM
    scale = HEAD_DIM ** (-0.5)
    query_heads = query_rows.reshape(frames_here, heads_here, HEAD_DIM)
    grad_heads = head_grad.reshape(frames_here, heads_here, HEAD_DIM)
    block_place = lax.axis_index("ctx")
    block_count = frame_lengths.shape[0]
    window = REACH * frames_here
    local_rows = jnp.arange(frames_here, dtype=jnp.int32)
    query_place = block_place * frames_here + local_rows

    def live_mask(offset):
        neighbour = block_place + offset
        key_place = neighbour * frames_here + local_rows
        limit = frame_lengths[jnp.clip(neighbour, 0, block_count - 1)]
        inside = (neighbour >= 0) & (neighbour < block_count)
        near = jnp.abs(query_place[:, None] - key_place[None, :]) <= window
        return near & (local_rows[None, :] < limit) & inside

    fetched = {0: (key_rows, value_rows)}
    for direction in (1, -1):
        last_key, last_value = (key_rows, value_rows)
        for distance in range(1, REACH + 1):
            send_key = last_key
            send_value = last_value
            last_key, last_value = shifted((send_key, send_value), "ctx", direction)
            fetched[-direction * distance] = (last_key, last_value)
    order = [0] + [offset for offset in range(-REACH, REACH + 1) if offset != 0]

    def block_logits(offset):
        keys_now = fetched[offset][0].reshape(frames_here, heads_here, HEAD_DIM)
        raw = (
            jnp.einsum("qhd,khd->hqk", query_heads, keys_now, preferred_element_type=jnp.float32)
            * scale
        )
        return jnp.where(live_mask(offset)[None], raw, -jnp.inf)

    def block_slopes(offset):
        values_now = fetched[offset][1].reshape(frames_here, heads_here, HEAD_DIM)
        return jnp.einsum(
            "qhd,khd->hqk", grad_heads, values_now, preferred_element_type=jnp.float32
        )

    for offset in order:
        logits = block_logits(offset)
        slopes = block_slopes(offset)
        if offset == 0:
            highest = jnp.max(logits, axis=2)
            scaled = jnp.exp(logits - highest[:, :, None])
            mass = jnp.sum(scaled, axis=2)
            weighted = jnp.sum(scaled * slopes, axis=2)
        else:
            fresh = jnp.maximum(highest, jnp.max(logits, axis=2))
            factor = jnp.exp(highest - fresh)
            scaled = jnp.exp(logits - fresh[:, :, None])
            mass = mass * factor + jnp.sum(scaled, axis=2)
            weighted = weighted * factor + jnp.sum(scaled * slopes, axis=2)
            highest = fresh
    log_total = highest + jnp.log(mass)
    delta = weighted / mass
    query_grad = jnp.zeros((frames_here, heads_here, HEAD_DIM), jnp.float32)
    for offset in order:
        keys_now = fetched[offset][0].reshape(frames_here, heads_here, HEAD_DIM)
        logits = block_logits(offset)
        probs = jnp.exp(logits - log_total[:, :, None])
        slopes = block_slopes(offset)
        dlogits = (probs * (slopes - delta[:, :, None])).astype(jnp.bfloat16)
        probs_low = probs.astype(jnp.bfloat16)
        query_grad = (
            query_grad
            + jnp.einsum("hqk,khd->qhd", dlogits, keys_now, preferred_element_type=jnp.float32)
            * scale
        )
        key_part = (
            (
                jnp.einsum("hqk,qhd->khd", dlogits, query_heads, preferred_element_type=jnp.float32)
                * scale
            )
            .astype(jnp.bfloat16)
            .reshape(frames_here, width_here)
        )
        value_part = (
            jnp.einsum("hqk,qhd->khd", probs_low, grad_heads, preferred_element_type=jnp.float32)
            .astype(jnp.bfloat16)
            .reshape(frames_here, width_here)
        )
        if offset == 0:
            key_total = key_part.astype(jnp.float32)
            value_total = value_part.astype(jnp.float32)
        else:
            back_key, back_value = shifted((key_part, value_part), "ctx", offset)
            key_total = key_total + back_key.astype(jnp.float32)
            value_total = value_total + back_value.astype(jnp.float32)
    return (
        d_resid_out,
        query_grad.reshape(frames_here, width_here).astype(jnp.bfloat16)[None],
        key_total.astype(jnp.bfloat16)[None],
        value_total.astype(jnp.bfloat16)[None],
    )


def solution(mesh):
    in_specs = (
        P("ctx", "head", None),
        P("ctx", "head", None),
        P("ctx", "head", None),
        P("ctx", "head", None),
        P("ctx", "head", None),
        P(),
        P(),
        P(),
    )
    out_specs = (
        P("ctx", None, "head"),
        P("ctx", None, "head"),
        P("ctx", None, "head"),
        P("ctx", None, "head"),
    )
    return jax.shard_map(
        on_device, mesh=mesh, in_specs=in_specs, out_specs=out_specs, check_vma=False
    )
```

profile of v0, /device:TPU:14, one launch (start us, length us, event | category | flops | bytes accessed | tf_op | source)
XLA Modules:
  0.0 204.8 jit_solution(15611372679468310429)
XLA Ops:
  7.2 1.2 copy.117
  8.9 1.4 reduce.3
  11.0 3.8 %all-to-all-start.2 = ((bf16[4,2,8192]{2,1,0:T(2,128)(2,1)}), bf16[4,2,8192]{2,1,0:T(2,128)(2,1)S(1)}, u32[]{:S(2)}, u32[]{:S(2)}) async-start(bf16[4,2,8192]{2,1,0:T(2,128)(2,1)} %reshape.507), calls=%async_computation.2 | async-start | bytes 262144 | tf_op jit(solution)/shard_map/all_to_all | solution.py:59
  14.8 1.5 fusion.111
  17.0 1.3 iota_compare_fusion.2
  18.3 1.3 iota_compare_fusion
  19.6 3.0 %fusion.33 = (pred[512,512]{0,1:T(8,128)(4,1)}, pred[512,512]{0,1:T(8,128)(4,1)}, pred[512,512]{0,1:T(8,128)(4,1)}, pred[512,512]{0,1:T(8,128)(4,1)}, pred[512,512]{0,1:T(8,128)(4,1)}) fusion(s32[512]{0:T(512)S(1)} %get-tuple-element.108, s32[512]{0:T(512)S(1)} %iota_add_fusion.4, pred[512]{0:T(512)(128)(4,1)S(1)} %get-tuple-element.106, pred[]{:T(512)S(6)} %and.169, ...), kind=kLoop, calls=%fused_computation.72 | loop fusion | flops 6553600 | bytes 1323525 | tf_op jit(solution)/shard_map/and | solution.py:110
  22.8 1.4 reduce.2
  25.0 1.4 reduce.4
  27.2 3.4 %all-to-all-start.3 = ((bf16[4,2,8192]{2,1,0:T(2,128)(2,1)}), bf16[4,2,8192]{2,1,0:T(2,128)(2,1)S(1)}, u32[]{:S(2)}, u32[]{:S(2)}) async-start(bf16[4,2,8192]{2,1,0:T(2,128)(2,1)} %reshape.503), calls=%async_computation.3 | async-start | bytes 262144 | tf_op jit(solution)/shard_map/all_to_all | solution.py:60
  31.3 2.2 %all-to-all-done.3 = bf16[4,2,8192]{2,1,0:T(2,128)(2,1)S(1)} async-done(((bf16[4,2,8192]{2,1,0:T(2,128)(2,1)}), bf16[4,2,8192]{2,1,0:T(2,128)(2,1)S(1)}, u32[]{:S(2)}, u32[]{:S(2)}) %all-to-all-start.3) | async-done | bytes 131104 | tf_op jit(solution)/shard_map/all_to_all | solution.py:60
  33.5 5.0 %all-to-all-start.4 = ((bf16[4,2,8192]{2,1,0:T(2,128)(2,1)}), bf16[4,2,8192]{2,1,0:T(2,128)(2,1)S(1)}, u32[]{:S(2)}, u32[]{:S(2)}) async-start(bf16[4,2,8192]{2,1,0:T(2,128)(2,1)} %reshape.505), calls=%async_computation.4 | async-start | bytes 262144 | tf_op jit(solution)/shard_map/all_to_all | solution.py:61
  38.9 2.2 %reduce.1 = bf16[1024,128]{1,0:T(8,128)(2,1)S(1)} reduce(bf16[1024,1,128]{2,1,0:T(2,128)(2,1)S(1)} %bitcast.177, bf16[]{:T(256)} %broadcast.279), dimensions={1}, to_apply=%bitcast.110.reduce_sub_computation | reduce | bytes 524290
  42.3 2.2 %reduce = bf16[1024,128]{1,0:T(8,128)(2,1)S(1)} reduce(bf16[1024,1,128]{2,1,0:T(2,128)(2,1)S(1)} %bitcast.176, bf16[]{:T(256)} %broadcast.279), dimensions={1}, to_apply=%bitcast.108.reduce_sub_computation | reduce | bytes 524290
  45.3 3.4 %all-to-all-start.1 = ((bf16[4,2,16384]{2,1,0:T(2,128)(2,1)}), bf16[4,2,16384]{2,1,0:T(2,128)(2,1)S(1)}, u32[]{:S(2)}, u32[]{:S(2)}) async-start(bf16[4,2,16384]{2,1,0:T(2,128)(2,1)} %reshape.501), calls=%async_computation.1 | async-start | bytes 524288 | tf_op jit(solution)/shard_map/all_to_all | solution.py:62
  49.7 2.4 %collective-permute-start.6 = (bf16[512,128]{1,0:T(8,128)(2,1)}, bf16[512,128]{1,0:T(8,128)(2,1)}, u32[]{:S(2)}, u32[]{:S(2)}) collective-permute-start(bf16[512,128]{1,0:T(8,128)(2,1)} %bitcast.40), channel_id=1, source_target_pairs={{1,0},{2,1},{3,2},{4,3},{5,4},{6,5},{7,6},{9,8},{10,9},{11,10},{12... | collective-permute-start | bytes 393224 | tf_op jit(solution)/shard_map/ppermute | solution.py:31
  52.2 4.3 %collective-permute-start.4 = (bf16[512,128]{1,0:T(8,128)(2,1)}, bf16[512,128]{1,0:T(8,128)(2,1)}, u32[]{:S(2)}, u32[]{:S(2)}) collective-permute-start(bf16[512,128]{1,0:T(8,128)(2,1)} %bitcast.40), channel_id=1, source_target_pairs={{0,1},{1,2},{2,3},{3,4},{4,5},{5,6},{6,7},{8,9},{9,10},{10,11},{11... | collective-permute-start | bytes 393224 | tf_op jit(solution)/shard_map/ppermute | solution.py:31
  57.8 1.9 collective-permute-start.10
  59.8 3.4 %all-to-all-start = ((bf16[4,2,16384]{2,1,0:T(2,128)(2,1)}), bf16[4,2,16384]{2,1,0:T(2,128)(2,1)S(1)}, u32[]{:S(2)}, u32[]{:S(2)}) async-start(bf16[4,2,16384]{2,1,0:T(2,128)(2,1)} %reshape.499), calls=%async_computation | async-start | bytes 524288 | tf_op jit(solution)/shard_map/all_to_all | solution.py:63
  63.7 4.8 %collective-permute-start.2 = (bf16[30,256]{1,0:T(8,128)(2,1)S(1)}, bf16[30,256]{1,0:T(8,128)(2,1)S(1)}, u32[]{:S(2)}, u32[]{:S(2)}) collective-permute-start(bf16[30,256]{1,0:T(8,128)(2,1)S(1)} %get-tuple-element.36), channel_id=1, source_target_pairs={{0,1},{1,2},{2,3},{3,4},{4,5},{5,6},{6,7},{8,9},{9,10},{10,11},{11... | collective-permute-start | bytes 46088 | tf_op jit(solution)/shard_map/ppermute | solution.py:19
  68.6 1.9 collective-permute-start.3
  71.0 4.8 %collective-permute-start = (bf16[30,256]{1,0:T(8,128)(2,1)S(1)}, bf16[30,256]{1,0:T(8,128)(2,1)S(1)}, u32[]{:S(2)}, u32[]{:S(2)}) collective-permute-start(bf16[30,256]{1,0:T(8,128)(2,1)S(1)} %get-tuple-element.38), channel_id=1, source_target_pairs={{0,1},{1,2},{2,3},{3,4},{4,5},{5,6},{6,7},{8,9},{9,10},{10,11},{11... | collective-permute-start | bytes 46088 | tf_op jit(solution)/shard_map/ppermute | solution.py:19
  75.8 1.9 collective-permute-start.1
  77.9 5.0 %collective-permute-start.8 = (bf16[512,128]{1,0:T(8,128)(2,1)}, bf16[512,128]{1,0:T(8,128)(2,1)}, u32[]{:S(2)}, u32[]{:S(2)}) collective-permute-start(bf16[512,128]{1,0:T(8,128)(2,1)} %bitcast.50), channel_id=1, source_target_pairs={{0,1},{1,2},{2,3},{3,4},{4,5},{5,6},{6,7},{8,9},{9,10},{10,11},{11... | collective-permute-start | bytes 393224 | tf_op jit(solution)/shard_map/ppermute | solution.py:31
  82.9 2.4 %slice_multiply_fusion.31 = f32[542,256]{1,0:T(8,128)S(1)} fusion(f32[572,256]{1,0:T(8,128)S(1)} %maximum_convert_fusion, f32[572,256]{1,0:T(8,128)S(1)} %maximum_convert_fusion.1, f32[256]{0:T(256)S(1)} %bitcast.221, f32[256]{0:T(256)S(1)} %bitcast.223, f32[256]{0:T(256)S(1)} %bitcast.225, f32[256]{0:T(256)S(1)} %bitcast.227, f32[256]{0:T(256)S(1)} %bitcast.229, ...), kind=kLoop, calls=%fused_computation.140 | loop fusion | flops 9573888 | bytes 18347008 | tf_op jit(solution)/shard_map/mul | solution.py:46
  85.4 2.8 %fusion.71 = bf16[512,256]{1,0:T(8,128)(2,1)} fusion(f32[542,256]{1,0:T(8,128)S(1)} %slice_multiply_fusion.31, f32[572,256]{1,0:T(8,128)S(1)} %maximum_convert_fusion, f32[256]{0:T(256)S(1)} %bitcast.222, f32[256]{0:T(256)S(1)} %bitcast.224, f32[256]{0:T(256)S(1)} %bitcast.226, f32[256]{0:T(256)S(1)} %bitcast.228, f32[256]{0:T(256)S(1)} %bitcast.230, ...), kind=kLoop, calls=%fused_computation.143 | loop fusion | flops 8257536 | bytes 17071104 | tf_op jit(solution)/shard_map/convert_element_type | solution.py:51
  88.2 1.6 fusion.115
  91.0 1.9 collective-permute-start.7
  92.9 1.7 copy.123
  94.6 4.9 %collective-permute-start.5 = (bf16[512,128]{1,0:T(8,128)(2,1)}, bf16[512,128]{1,0:T(8,128)(2,1)}, u32[]{:S(2)}, u32[]{:S(2)}) collective-permute-start(bf16[512,128]{1,0:T(8,128)(2,1)} %collective-permute-done.4), channel_id=1, source_target_pairs={{0,1},{1,2},{2,3},{3,4},{4,5},{5,6},{6,7},{8,9},{9,10},{10,11},{11... | collective-permute-start | bytes 393224 | tf_op jit(solution)/shard_map/ppermute | solution.py:31
  99.6 1.9 collective-permute-start.11
  101.5 4.8 %collective-permute-start.9 = (bf16[512,128]{1,0:T(8,128)(2,1)}, bf16[512,128]{1,0:T(8,128)(2,1)}, u32[]{:S(2)}, u32[]{:S(2)}) collective-permute-start(bf16[512,128]{1,0:T(8,128)(2,1)} %collective-permute-done.8), channel_id=1, source_target_pairs={{0,1},{1,2},{2,3},{3,4},{4,5},{5,6},{6,7},{8,9},{9,10},{10,11},{11... | collective-permute-start | bytes 393224 | tf_op jit(solution)/shard_map/ppermute | solution.py:31
  106.4 3.5 %fusion.113 = (f32[2,512]{1,0:T(2,128)}, f32[2,512,512]{1,2,0:T(8,128)}) fusion(bf16[512,2,64]{0,2,1:T(8,128)(2,1)S(1)} %reshape_squeeze.12, bf16[512,2,64]{0,2,1:T(8,128)(2,1)S(1)} %bitcast.213, pred[512,512]{0,1:T(8,128)(4,1)} %get-tuple-element.78), kind=kOutput, calls=%fused_computation.237 | convolution fusion | flops 68680704 | bytes 2625536 | tf_op jit(solution)/shard_map/qhd,khd->hqk/dot_general | solution.py:125
  109.9 2.5 %fusion.114 = (f32[2,512]{1,0:T(2,128)}, f32[2,512,512]{1,2,0:T(8,128)}) fusion(bf16[512,2,64]{0,2,1:T(8,128)(2,1)S(1)} %reshape_squeeze.12, bf16[512,2,64]{0,2,1:T(8,128)(2,1)S(1)} %bitcast.217, pred[512,512]{0,1:T(8,128)(4,1)S(1)} %copy-done.27), kind=kOutput, calls=%fused_computation.238 | convolution fusion | flops 68680704 | bytes 2625536 | tf_op jit(solution)/shard_map/qhd,khd->hqk/dot_general | solution.py:125
  112.4 1.7 copy.131
  114.0 1.7 copy.130
  116.7 1.7 copy.122
  118.4 1.7 copy.132
  120.1 1.7 copy.129
  121.8 3.0 %fusion.116 = (f32[2,512]{1,0:T(2,128)S(1)}, f32[2,512,512]{1,2,0:T(8,128)}) fusion(bf16[512,2,64]{0,2,1:T(8,128)(2,1)S(1)} %reshape_squeeze.12, bf16[512,2,64]{0,2,1:T(8,128)(2,1)} %bitcast.215, pred[512,512]{0,1:T(8,128)(4,1)} %get-tuple-element.76), kind=kOutput, calls=%fused_computation.240 | convolution fusion | flops 68680704 | bytes 2625536 | tf_op jit(solution)/shard_map/qhd,khd->hqk/dot_general | solution.py:125
  124.8 2.0 fusion.112
  126.9 1.7 convolution_convert_fusion.5
  136.1 1.1 convolution_convert_fusion.2
  138.4 1.1 convolution_convert_fusion
  139.5 1.2 fusion.12
  140.7 4.3 %multiply_convert_fusion = (bf16[2,512,512]{1,2,0:T(8,128)(2,1)}, bf16[2,512,512]{1,2,0:T(8,128)(2,1)}, bf16[2,512,512]{1,2,0:T(8,128)(2,1)}, bf16[2,512,512]{1,2,0:T(8,128)(2,1)S(1)}, bf16[2,512,512]{1,2,0:T(8,128)(2,1)}) fusion(f32[2,512,512]{1,2,0:T(8,128)S(1)} %get-tuple-element.96, f32[2,512,512]{1,2,0:T(8,128)S(1)} %copy-done.4, ...), kind=kLoop, calls=%fused_computation | loop fusion | flops 10485760 | bytes 26222592 | tf_op jit(solution)/shard_map/convert_element_type | solution.py:159
  151.5 1.7 copy.147
  153.2 2.3 %fusion.15 = bf16[2,512,64]{1,2,0:T(8,128)(2,1)} fusion(bf16[2,512,512]{1,2,0:T(8,128)(2,1)} %get-tuple-element.72, bf16[512,2,64]{0,2,1:T(8,128)(2,1)S(1)} %reshape_squeeze.12), kind=kOutput, calls=%fused_computation.54 | convolution fusion | flops 67239936 | bytes 1310720 | tf_op jit(solution)/shard_map/hqk,qhd->khd/dot_general | solution.py:168
  155.5 1.7 copy.140
  157.2 2.3 %fusion.16 = bf16[2,512,64]{1,2,0:T(8,128)(2,1)} fusion(bf16[2,512,512]{1,2,0:T(8,128)(2,1)} %get-tuple-element.73, bf16[512,2,64]{0,2,1:T(8,128)(2,1)S(1)} %reshape_squeeze.12), kind=kOutput, calls=%fused_computation.55 | convolution fusion | flops 67239936 | bytes 1310720 | tf_op jit(solution)/shard_map/hqk,qhd->khd/dot_general | solution.py:168
  159.5 1.6 copy.143
  161.1 1.7 copy.145
  162.8 1.3 fusion.117
  164.1 1.6 convolution_add_fusion.2
  167.1 1.7 copy.158
  168.7 2.0 collective-permute-start.14
  170.8 3.8 %collective-permute-start.13 = (bf16[512,128]{1,0:T(8,128)(2,1)}, bf16[512,128]{1,0:T(8,128)(2,1)S(1)}, u32[]{:S(2)}, u32[]{:S(2)}) collective-permute-start(bf16[512,128]{1,0:T(8,128)(2,1)} %copy.143), channel_id=1, source_target_pairs={{1,0},{2,1},{3,2},{4,3},{5,4},{6,5},{7,6},{9,8},{10,9},{11,10},{12... | collective-permute-start | bytes 393224 | tf_op jit(solution)/shard_map/ppermute | solution.py:31
  174.6 2.4 %collective-permute-start.12 = (bf16[512,128]{1,0:T(8,128)(2,1)}, bf16[512,128]{1,0:T(8,128)(2,1)S(1)}, u32[]{:S(2)}, u32[]{:S(2)}) collective-permute-start(bf16[512,128]{1,0:T(8,128)(2,1)} %copy.140), channel_id=1, source_target_pairs={{2,0},{3,1},{4,2},{5,3},{6,4},{7,5},{10,8},{11,9},{12,10},{13,11},... | collective-permute-start | bytes 393224 | tf_op jit(solution)/shard_map/ppermute | solution.py:31
  177.0 3.5 %collective-permute-start.15 = (bf16[512,128]{1,0:T(8,128)(2,1)}, bf16[512,128]{1,0:T(8,128)(2,1)S(1)}, u32[]{:S(2)}, u32[]{:S(2)}) collective-permute-start(bf16[512,128]{1,0:T(8,128)(2,1)} %copy.147), channel_id=1, source_target_pairs={{0,2},{1,3},{2,4},{3,5},{4,6},{5,7},{8,10},{9,11},{10,12},{11,13},... | collective-permute-start | bytes 393224 | tf_op jit(solution)/shard_map/ppermute | solution.py:31
  181.0 2.4 %collective-permute-start.16 = (bf16[512,128]{1,0:T(8,128)(2,1)}, bf16[512,128]{1,0:T(8,128)(2,1)S(1)}, u32[]{:S(2)}, u32[]{:S(2)}) collective-permute-start(bf16[512,128]{1,0:T(8,128)(2,1)} %copy.150), channel_id=1, source_target_pairs={{2,0},{3,1},{4,2},{5,3},{6,4},{7,5},{10,8},{11,9},{12,10},{13,11},... | collective-permute-start | bytes 393224 | tf_op jit(solution)/shard_map/ppermute | solution.py:31
  183.4 1.9 collective-permute-start.17
  185.3 4.8 %collective-permute-start.18 = (bf16[512,128]{1,0:T(8,128)(2,1)}, bf16[512,128]{1,0:T(8,128)(2,1)S(1)}, u32[]{:S(2)}, u32[]{:S(2)}) collective-permute-start(bf16[512,128]{1,0:T(8,128)(2,1)} %copy.155), channel_id=1, source_target_pairs={{0,1},{1,2},{2,3},{3,4},{4,5},{5,6},{6,7},{8,9},{9,10},{10,11},{11... | collective-permute-start | bytes 393224 | tf_op jit(solution)/shard_map/ppermute | solution.py:31
  190.2 3.5 %collective-permute-start.19 = (bf16[512,128]{1,0:T(8,128)(2,1)}, bf16[512,128]{1,0:T(8,128)(2,1)S(1)}, u32[]{:S(2)}, u32[]{:S(2)}) collective-permute-start(bf16[512,128]{1,0:T(8,128)(2,1)} %copy.157), channel_id=1, source_target_pairs={{0,2},{1,3},{2,4},{3,5},{4,6},{5,7},{8,10},{9,11},{10,12},{11,13},... | collective-permute-start | bytes 393224 | tf_op jit(solution)/shard_map/ppermute | solution.py:31
  194.4 2.8 %collective-permute-done.19 = bf16[512,128]{1,0:T(8,128)(2,1)S(1)} collective-permute-done((bf16[512,128]{1,0:T(8,128)(2,1)}, bf16[512,128]{1,0:T(8,128)(2,1)S(1)}, u32[]{:S(2)}, u32[]{:S(2)}) %collective-permute-start.19) | collective-permute-done | bytes 131104 | tf_op jit(solution)/shard_map/ppermute | solution.py:31
  (161 shorter events, 30.7 us)
Async XLA Ops:
  7.2 119.7 %copy-start = (bf16[512,1024]{1,0:T(8,128)(2,1)S(1)}, bf16[512,1024]{1,0:T(8,128)(2,1)}, u32[]{:S(2)}) copy-start(bf16[512,1024]{1,0:T(8,128)(2,1)} %param.13) | copy-start | bytes 3145732
  7.2 15.4 %copy-start.28 = (bf16[1,128,512]{2,1,0:T(8,128)(2,1)S(1)}, bf16[1,128,512]{2,1,0:T(8,128)(2,1)}, u32[]{:S(2)}) copy-start(bf16[1,128,512]{2,1,0:T(8,128)(2,1)} %param.9) | copy-start | bytes 393220
  7.2 17.7 %copy-start.29 = (bf16[1,128,512]{2,1,0:T(8,128)(2,1)S(1)}, bf16[1,128,512]{2,1,0:T(8,128)(2,1)}, u32[]{:S(2)}) copy-start(bf16[1,128,512]{2,1,0:T(8,128)(2,1)} %param.10) | copy-start | bytes 393220
  11.0 16.2 %all-to-all-start.2 = ((bf16[4,2,8192]{2,1,0:T(2,128)(2,1)}), bf16[4,2,8192]{2,1,0:T(2,128)(2,1)S(1)}, u32[]{:S(2)}, u32[]{:S(2)}) async-start(bf16[4,2,8192]{2,1,0:T(2,128)(2,1)} %reshape.507), calls=%async_computation.2 | async-start | bytes 262144 | tf_op jit(solution)/shard_map/all_to_all | solution.py:59
  14.8 23.7 %copy-start.24 = (bf16[1,128,1024]{2,1,0:T(8,128)(2,1)S(1)}, bf16[1,128,1024]{2,1,0:T(8,128)(2,1)}, u32[]{:S(2)}) copy-start(bf16[1,128,1024]{2,1,0:T(8,128)(2,1)} %param.11) | copy-start | bytes 786436
  24.2 17.7 %copy-start.25 = (bf16[1,128,1024]{2,1,0:T(8,128)(2,1)S(1)}, bf16[1,128,1024]{2,1,0:T(8,128)(2,1)}, u32[]{:S(2)}) copy-start(bf16[1,128,1024]{2,1,0:T(8,128)(2,1)} %param.12) | copy-start | bytes 786436
  27.2 6.4 %all-to-all-start.3 = ((bf16[4,2,8192]{2,1,0:T(2,128)(2,1)}), bf16[4,2,8192]{2,1,0:T(2,128)(2,1)S(1)}, u32[]{:S(2)}, u32[]{:S(2)}) async-start(bf16[4,2,8192]{2,1,0:T(2,128)(2,1)} %reshape.503), calls=%async_computation.3 | async-start | bytes 262144 | tf_op jit(solution)/shard_map/all_to_all | solution.py:60
  33.5 11.8 %all-to-all-start.4 = ((bf16[4,2,8192]{2,1,0:T(2,128)(2,1)}), bf16[4,2,8192]{2,1,0:T(2,128)(2,1)S(1)}, u32[]{:S(2)}, u32[]{:S(2)}) async-start(bf16[4,2,8192]{2,1,0:T(2,128)(2,1)} %reshape.505), calls=%async_computation.4 | async-start | bytes 262144 | tf_op jit(solution)/shard_map/all_to_all | solution.py:61
  45.3 14.5 %all-to-all-start.1 = ((bf16[4,2,16384]{2,1,0:T(2,128)(2,1)}), bf16[4,2,16384]{2,1,0:T(2,128)(2,1)S(1)}, u32[]{:S(2)}, u32[]{:S(2)}) async-start(bf16[4,2,16384]{2,1,0:T(2,128)(2,1)} %reshape.501), calls=%async_computation.1 | async-start | bytes 524288 | tf_op jit(solution)/shard_map/all_to_all | solution.py:62
  49.7 40.2 %collective-permute-start.6 = (bf16[512,128]{1,0:T(8,128)(2,1)}, bf16[512,128]{1,0:T(8,128)(2,1)}, u32[]{:S(2)}, u32[]{:S(2)}) collective-permute-start(bf16[512,128]{1,0:T(8,128)(2,1)} %bitcast.40), channel_id=1, source_target_pairs={{1,0},{2,1},{3,2},{4,3},{5,4},{6,5},{7,6},{9,8},{10,9},{11,10},{12... | collective-permute-start | bytes 393224 | tf_op jit(solution)/shard_map/ppermute | solution.py:31
  52.2 40.8 %collective-permute-start.4 = (bf16[512,128]{1,0:T(8,128)(2,1)}, bf16[512,128]{1,0:T(8,128)(2,1)}, u32[]{:S(2)}, u32[]{:S(2)}) collective-permute-start(bf16[512,128]{1,0:T(8,128)(2,1)} %bitcast.40), channel_id=1, source_target_pairs={{0,1},{1,2},{2,3},{3,4},{4,5},{5,6},{6,7},{8,9},{9,10},{10,11},{11... | collective-permute-start | bytes 393224 | tf_op jit(solution)/shard_map/ppermute | solution.py:31
  56.9 31.3 %copy-start.19 = (bf16[512,2,64]{0,2,1:T(8,128)(2,1)}, bf16[512,2,64]{0,2,1:T(8,128)(2,1)S(1)}, u32[]{:S(2)}) copy-start(bf16[512,2,64]{0,2,1:T(8,128)(2,1)S(1)} %reshape_squeeze.13) | copy-start | bytes 393220
  57.8 41.7 %collective-permute-start.10 = (bf16[512,128]{1,0:T(8,128)(2,1)}, bf16[512,128]{1,0:T(8,128)(2,1)}, u32[]{:S(2)}, u32[]{:S(2)}) collective-permute-start(bf16[512,128]{1,0:T(8,128)(2,1)} %bitcast.50), channel_id=1, source_target_pairs={{1,0},{2,1},{3,2},{4,3},{5,4},{6,5},{7,6},{9,8},{10,9},{11,10},{12... | collective-permute-start | bytes 393224 | tf_op jit(solution)/shard_map/ppermute | solution.py:31
  59.8 10.7 %all-to-all-start = ((bf16[4,2,16384]{2,1,0:T(2,128)(2,1)}), bf16[4,2,16384]{2,1,0:T(2,128)(2,1)S(1)}, u32[]{:S(2)}, u32[]{:S(2)}) async-start(bf16[4,2,16384]{2,1,0:T(2,128)(2,1)} %reshape.499), calls=%async_computation | async-start | bytes 524288 | tf_op jit(solution)/shard_map/all_to_all | solution.py:63
  63.2 63.7 %all-gather.2.cloned.1.call-start = ((), (), s32[]{:S(2)}) async-start(), calls=%async_computation.5 | async-start | bytes 1310720 | tf_op jit(solution)/shard_map/all_gather | solution.py:85
  63.7 7.3 %collective-permute-start.2 = (bf16[30,256]{1,0:T(8,128)(2,1)S(1)}, bf16[30,256]{1,0:T(8,128)(2,1)S(1)}, u32[]{:S(2)}, u32[]{:S(2)}) collective-permute-start(bf16[30,256]{1,0:T(8,128)(2,1)S(1)} %get-tuple-element.36), channel_id=1, source_target_pairs={{0,1},{1,2},{2,3},{3,4},{4,5},{5,6},{6,7},{8,9},{9,10},{10,11},{11... | collective-permute-start | bytes 46088 | tf_op jit(solution)/shard_map/ppermute | solution.py:19
  68.6 7.3 %collective-permute-start.3 = (bf16[30,256]{1,0:T(8,128)(2,1)S(1)}, bf16[30,256]{1,0:T(8,128)(2,1)S(1)}, u32[]{:S(2)}, u32[]{:S(2)}) collective-permute-start(bf16[30,256]{1,0:T(8,128)(2,1)S(1)} %get-tuple-element.37), channel_id=1, source_target_pairs={{1,0},{2,1},{3,2},{4,3},{5,4},{6,5},{7,6},{9,8},{10,9},{11,10},{12... | collective-permute-start | bytes 46088 | tf_op jit(solution)/shard_map/ppermute | solution.py:21
  71.0 6.8 %collective-permute-start = (bf16[30,256]{1,0:T(8,128)(2,1)S(1)}, bf16[30,256]{1,0:T(8,128)(2,1)S(1)}, u32[]{:S(2)}, u32[]{:S(2)}) collective-permute-start(bf16[30,256]{1,0:T(8,128)(2,1)S(1)} %get-tuple-element.38), channel_id=1, source_target_pairs={{0,1},{1,2},{2,3},{3,4},{4,5},{5,6},{6,7},{8,9},{9,10},{10,11},{11... | collective-permute-start | bytes 46088 | tf_op jit(solution)/shard_map/ppermute | solution.py:19
  75.8 7.0 %collective-permute-start.1 = (bf16[30,256]{1,0:T(8,128)(2,1)S(1)}, bf16[30,256]{1,0:T(8,128)(2,1)S(1)}, u32[]{:S(2)}, u32[]{:S(2)}) collective-permute-start(bf16[30,256]{1,0:T(8,128)(2,1)S(1)} %get-tuple-element.39), channel_id=1, source_target_pairs={{1,0},{2,1},{3,2},{4,3},{5,4},{6,5},{7,6},{9,8},{10,9},{11,10},{12... | collective-permute-start | bytes 46088 | tf_op jit(solution)/shard_map/ppermute | solution.py:21
  77.9 23.7 %collective-permute-start.8 = (bf16[512,128]{1,0:T(8,128)(2,1)}, bf16[512,128]{1,0:T(8,128)(2,1)}, u32[]{:S(2)}, u32[]{:S(2)}) collective-permute-start(bf16[512,128]{1,0:T(8,128)(2,1)} %bitcast.50), channel_id=1, source_target_pairs={{0,1},{1,2},{2,3},{3,4},{4,5},{5,6},{6,7},{8,9},{9,10},{10,11},{11... | collective-permute-start | bytes 393224 | tf_op jit(solution)/shard_map/ppermute | solution.py:31
  91.0 21.4 %copy-start.20 = (bf16[512,128]{0,1:T(8,128)(2,1)}, bf16[512,128]{0,1:T(8,128)(2,1)S(1)}, u32[]{:S(2)}) copy-start(bf16[512,128]{0,1:T(8,128)(2,1)S(1)} %copy.124) | copy-start | bytes 393220
  91.0 24.7 %collective-permute-start.7 = (bf16[512,128]{1,0:T(8,128)(2,1)}, bf16[512,128]{1,0:T(8,128)(2,1)}, u32[]{:S(2)}, u32[]{:S(2)}) collective-permute-start(bf16[512,128]{1,0:T(8,128)(2,1)} %collective-permute-done.6), channel_id=1, source_target_pairs={{1,0},{2,1},{3,2},{4,3},{5,4},{6,5},{7,6},{9,8},{10,9},{11,10},{12... | collective-permute-start | bytes 393224 | tf_op jit(solution)/shard_map/ppermute | solution.py:31
  94.6 15.2 %copy-start.22 = (bf16[512,128]{0,1:T(8,128)(2,1)S(1)}, bf16[512,128]{0,1:T(8,128)(2,1)}, u32[]{:S(2)}) copy-start(bf16[512,128]{0,1:T(8,128)(2,1)} %copy.123) | copy-start | bytes 393220
  94.6 15.2 %copy-start.27 = (pred[512,512]{0,1:T(8,128)(4,1)S(1)}, pred[512,512]{0,1:T(8,128)(4,1)}, u32[]{:S(2)}) copy-start(pred[512,512]{0,1:T(8,128)(4,1)} %get-tuple-element.77) | copy-start | bytes 786436
  94.6 22.1 %collective-permute-start.5 = (bf16[512,128]{1,0:T(8,128)(2,1)}, bf16[512,128]{1,0:T(8,128)(2,1)}, u32[]{:S(2)}, u32[]{:S(2)}) collective-permute-start(bf16[512,128]{1,0:T(8,128)(2,1)} %collective-permute-done.4), channel_id=1, source_target_pairs={{0,1},{1,2},{2,3},{3,4},{4,5},{5,6},{6,7},{8,9},{9,10},{10,11},{11... | collective-permute-start | bytes 393224 | tf_op jit(solution)/shard_map/ppermute | solution.py:31
  99.6 18.9 %collective-permute-start.11 = (bf16[512,128]{1,0:T(8,128)(2,1)}, bf16[512,128]{1,0:T(8,128)(2,1)}, u32[]{:S(2)}, u32[]{:S(2)}) collective-permute-start(bf16[512,128]{1,0:T(8,128)(2,1)} %collective-permute-done.10), channel_id=1, source_target_pairs={{1,0},{2,1},{3,2},{4,3},{5,4},{6,5},{7,6},{9,8},{10,9},{11,10},{12... | collective-permute-start | bytes 393224 | tf_op jit(solution)/shard_map/ppermute | solution.py:31
  101.5 18.6 %collective-permute-start.9 = (bf16[512,128]{1,0:T(8,128)(2,1)}, bf16[512,128]{1,0:T(8,128)(2,1)}, u32[]{:S(2)}, u32[]{:S(2)}) collective-permute-start(bf16[512,128]{1,0:T(8,128)(2,1)} %collective-permute-done.8), channel_id=1, source_target_pairs={{0,1},{1,2},{2,3},{3,4},{4,5},{5,6},{6,7},{8,9},{9,10},{10,11},{11... | collective-permute-start | bytes 393224 | tf_op jit(solution)/shard_map/ppermute | solution.py:31
  116.7 10.1 %copy-start.10 = (bf16[512,128]{0,1:T(8,128)(2,1)}, bf16[512,128]{0,1:T(8,128)(2,1)S(1)}, u32[]{:S(2)}) copy-start(bf16[512,128]{0,1:T(8,128)(2,1)S(1)} %copy.125) | copy-start | bytes 393220
  121.8 3.0 %copy-start.26 = (pred[512,512]{0,1:T(8,128)(4,1)S(1)}, pred[512,512]{0,1:T(8,128)(4,1)}, u32[]{:S(2)}) copy-start(pred[512,512]{0,1:T(8,128)(4,1)} %get-tuple-element.79) | copy-start | bytes 786436
  121.8 5.1 %copy-start.32 = (f32[2,512]{1,0:T(2,128)S(1)}, f32[2,512]{1,0:T(2,128)}, u32[]{:S(2)}) copy-start(f32[2,512]{1,0:T(2,128)} %get-tuple-element.88) | copy-start | bytes 12292
  121.8 5.1 %copy-start.33 = (f32[2,512]{1,0:T(2,128)S(1)}, f32[2,512]{1,0:T(2,128)}, u32[]{:S(2)}) copy-start(f32[2,512]{1,0:T(2,128)} %get-tuple-element.90) | copy-start | bytes 12292
  126.9 8.8 %copy-start.30 = (f32[2,512]{1,0:T(2,128)}, f32[2,512]{1,0:T(2,128)S(1)}, u32[]{:S(2)}) copy-start(f32[2,512]{1,0:T(2,128)S(1)} %get-tuple-element.35) | copy-start | bytes 12292
  128.6 1.6 copy-start.4
  128.6 1.6 copy-start.18
  130.2 1.6 copy-start.1
  130.2 1.6 copy-start.13
  131.8 1.6 copy-start.2
  131.8 1.6 copy-start.12
  133.4 1.6 copy-start.3
  133.4 1.6 copy-start.14
  138.4 2.3 %copy-start.31 = (f32[2,512]{1,0:T(2,128)S(1)}, f32[2,512]{1,0:T(2,128)}, u32[]{:S(2)}) copy-start(f32[2,512]{1,0:T(2,128)} %copy-done.30) | copy-start | bytes 12292
  140.7 5.4 %copy-start.21 = (bf16[512,128]{0,1:T(8,128)(2,1)S(1)}, bf16[512,128]{0,1:T(8,128)(2,1)}, u32[]{:S(2)}) copy-start(bf16[512,128]{0,1:T(8,128)(2,1)} %copy-done.20) | copy-start | bytes 393220
  145.0 2.2 %copy-start.8 = (f32[2,64,512]{2,1,0:T(8,128)S(1)}, f32[2,64,512]{2,1,0:T(8,128)}, u32[]{:S(2)}) copy-start(f32[2,64,512]{2,1,0:T(8,128)} %fusion.12) | copy-start | bytes 786436
  145.0 2.3 %copy-start.17 = (bf16[2,64,512]{2,1,0:T(8,128)(2,1)S(1)}, bf16[2,64,512]{2,1,0:T(8,128)(2,1)}, u32[]{:S(2)}) copy-start(bf16[2,64,512]{2,1,0:T(8,128)(2,1)} %convolution_convert_fusion) | copy-start | bytes 393220
  145.0 3.1 %copy-start.16 = (bf16[2,64,512]{2,1,0:T(8,128)(2,1)S(1)}, bf16[2,64,512]{2,1,0:T(8,128)(2,1)}, u32[]{:S(2)}) copy-start(bf16[2,64,512]{2,1,0:T(8,128)(2,1)} %convolution_convert_fusion.1) | copy-start | bytes 393220
  145.0 3.8 %copy-start.15 = (bf16[2,64,512]{2,1,0:T(8,128)(2,1)S(1)}, bf16[2,64,512]{2,1,0:T(8,128)(2,1)}, u32[]{:S(2)}) copy-start(bf16[2,64,512]{2,1,0:T(8,128)(2,1)} %convolution_convert_fusion.2) | copy-start | bytes 393220
  145.0 5.4 %copy-start.6 = (bf16[2,512,512]{1,2,0:T(8,128)(2,1)S(1)}, bf16[2,512,512]{1,2,0:T(8,128)(2,1)}, u32[]{:S(2)}) copy-start(bf16[2,512,512]{1,2,0:T(8,128)(2,1)} %get-tuple-element.71) | copy-start | bytes 3145732
  151.5 11.4 %copy-start.5 = (bf16[2,512,512]{1,2,0:T(8,128)(2,1)S(1)}, bf16[2,512,512]{1,2,0:T(8,128)(2,1)}, u32[]{:S(2)}) copy-start(bf16[2,512,512]{1,2,0:T(8,128)(2,1)} %get-tuple-element.75) | copy-start | bytes 3145732
  162.8 3.0 %copy-start.7 = (bf16[2,512,512]{1,2,0:T(8,128)(2,1)S(1)}, bf16[2,512,512]{1,2,0:T(8,128)(2,1)}, u32[]{:S(2)}) copy-start(bf16[2,512,512]{1,2,0:T(8,128)(2,1)} %get-tuple-element.73) | copy-start | bytes 3145732
  162.8 3.0 %copy-start.9 = (f32[2,512,64]{1,2,0:T(8,128)S(1)}, f32[2,512,64]{1,2,0:T(8,128)}, u32[]{:S(2)}) copy-start(f32[2,512,64]{1,2,0:T(8,128)} %fusion.118) | copy-start | bytes 786436
  162.8 3.0 %copy-start.23 = (bf16[512,128]{0,1:T(8,128)(2,1)S(1)}, bf16[512,128]{0,1:T(8,128)(2,1)}, u32[]{:S(2)}) copy-start(bf16[512,128]{0,1:T(8,128)(2,1)} %copy.123) | copy-start | bytes 393220
  164.1 2.0 copy-start.11
  168.7 14.6 %collective-permute-start.14 = (bf16[512,128]{1,0:T(8,128)(2,1)}, bf16[512,128]{1,0:T(8,128)(2,1)S(1)}, u32[]{:S(2)}, u32[]{:S(2)}) collective-permute-start(bf16[512,128]{1,0:T(8,128)(2,1)} %copy.145), channel_id=1, source_target_pairs={{0,1},{1,2},{2,3},{3,4},{4,5},{5,6},{6,7},{8,9},{9,10},{10,11},{11... | collective-permute-start | bytes 393224 | tf_op jit(solution)/shard_map/ppermute | solution.py:31
  170.8 14.6 %collective-permute-start.13 = (bf16[512,128]{1,0:T(8,128)(2,1)}, bf16[512,128]{1,0:T(8,128)(2,1)S(1)}, u32[]{:S(2)}, u32[]{:S(2)}) collective-permute-start(bf16[512,128]{1,0:T(8,128)(2,1)} %copy.143), channel_id=1, source_target_pairs={{1,0},{2,1},{3,2},{4,3},{5,4},{6,5},{7,6},{9,8},{10,9},{11,10},{12... | collective-permute-start | bytes 393224 | tf_op jit(solution)/shard_map/ppermute | solution.py:31
  174.6 15.6 %collective-permute-start.12 = (bf16[512,128]{1,0:T(8,128)(2,1)}, bf16[512,128]{1,0:T(8,128)(2,1)S(1)}, u32[]{:S(2)}, u32[]{:S(2)}) collective-permute-start(bf16[512,128]{1,0:T(8,128)(2,1)} %copy.140), channel_id=1, source_target_pairs={{2,0},{3,1},{4,2},{5,3},{6,4},{7,5},{10,8},{11,9},{12,10},{13,11},... | collective-permute-start | bytes 393224 | tf_op jit(solution)/shard_map/ppermute | solution.py:31
  177.0 16.7 %collective-permute-start.15 = (bf16[512,128]{1,0:T(8,128)(2,1)}, bf16[512,128]{1,0:T(8,128)(2,1)S(1)}, u32[]{:S(2)}, u32[]{:S(2)}) collective-permute-start(bf16[512,128]{1,0:T(8,128)(2,1)} %copy.147), channel_id=1, source_target_pairs={{0,2},{1,3},{2,4},{3,5},{4,6},{5,7},{8,10},{9,11},{10,12},{11,13},... | collective-permute-start | bytes 393224 | tf_op jit(solution)/shard_map/ppermute | solution.py:31
  181.0 13.4 %collective-permute-start.16 = (bf16[512,128]{1,0:T(8,128)(2,1)}, bf16[512,128]{1,0:T(8,128)(2,1)S(1)}, u32[]{:S(2)}, u32[]{:S(2)}) collective-permute-start(bf16[512,128]{1,0:T(8,128)(2,1)} %copy.150), channel_id=1, source_target_pairs={{2,0},{3,1},{4,2},{5,3},{6,4},{7,5},{10,8},{11,9},{12,10},{13,11},... | collective-permute-start | bytes 393224 | tf_op jit(solution)/shard_map/ppermute | solution.py:31
  183.4 11.0 %collective-permute-start.17 = (bf16[512,128]{1,0:T(8,128)(2,1)}, bf16[512,128]{1,0:T(8,128)(2,1)S(1)}, u32[]{:S(2)}, u32[]{:S(2)}) collective-permute-start(bf16[512,128]{1,0:T(8,128)(2,1)} %copy.153), channel_id=1, source_target_pairs={{1,0},{2,1},{3,2},{4,3},{5,4},{6,5},{7,6},{9,8},{10,9},{11,10},{12... | collective-permute-start | bytes 393224 | tf_op jit(solution)/shard_map/ppermute | solution.py:31
  185.3 9.1 %collective-permute-start.18 = (bf16[512,128]{1,0:T(8,128)(2,1)}, bf16[512,128]{1,0:T(8,128)(2,1)S(1)}, u32[]{:S(2)}, u32[]{:S(2)}) collective-permute-start(bf16[512,128]{1,0:T(8,128)(2,1)} %copy.155), channel_id=1, source_target_pairs={{0,1},{1,2},{2,3},{3,4},{4,5},{5,6},{6,7},{8,9},{9,10},{10,11},{11... | collective-permute-start | bytes 393224 | tf_op jit(solution)/shard_map/ppermute | solution.py:31
  190.2 7.1 %collective-permute-start.19 = (bf16[512,128]{1,0:T(8,128)(2,1)}, bf16[512,128]{1,0:T(8,128)(2,1)S(1)}, u32[]{:S(2)}, u32[]{:S(2)}) collective-permute-start(bf16[512,128]{1,0:T(8,128)(2,1)} %copy.157), channel_id=1, source_target_pairs={{0,2},{1,3},{2,4},{3,5},{4,6},{5,7},{8,10},{9,11},{10,12},{11,13},... | collective-permute-start | bytes 393224 | tf_op jit(solution)/shard_map/ppermute | solution.py:31
Sparse Core Ops, SparseCore 0:
  88.3 15.9 all-gather.1
where the time goes:
time: 207 us; the launch traced here: 205 us
  starting transfers between devices  84.1 us (41%)
  local copies, waits for them, and re-layouts  39.1 us (19%)
  matrix products  34.8 us (17%)
  other arithmetic  26.7 us (13%)
  between operations  14.9 us (7%)
  waiting for transfers between devices  5.17 us (2%)
    ppermute x16, starting transfers between devices, shifted(): lax.ppermute(value, axis, [(source, source + steps) for source in range(f...  51.5 us
    unnamed x90, local copies, waits for them, and re-layouts  13.2 us
    dot_general x5, matrix products, block_logits(): jnp.einsum('qhd,khd->hqk', query_heads, keys_now, preferred_element_type=...  12.6 us
    ppermute x8, local copies, waits for them, and re-layouts, shifted(): lax.ppermute(value, axis, [(source, source + steps) for source in range(f...  12 us
    ppermute x2, starting transfers between devices, padded(): lax.ppermute(tail, axis, [(i, (i + 1) % count) for i in range(ends)])  9.64 us
    unnamed x5, other arithmetic  8.65 us
    dot_general x5, matrix products, on_device(): jnp.einsum('hqk,qhd->khd', dlogits, query_heads, preferred_element_type=j...  7.3 us
    reshape x4, local copies, waits for them, and re-layouts, on_device(): key_part = (jnp.einsum('hqk,qhd->khd', dlogits, query_heads, preferred_el...  6.71 us
  transfers between devices with their start and end apart: 26, of which 2 were waited for; matrix products, arithmetic and copies ran while one was open for 27% of the time, Pallas kernels for 0%

commit v1 on v0

--- a/solution.py
+++ b/solution.py
@@ -6,6 +6,28 @@
 HEAD_DIM = 64
 KERNEL = 31
 REACH = 2
+
+
+def split_up(value, dim, size):
+    before, after = (value.shape[:dim], value.shape[dim + 1 :])
+    return jnp.moveaxis(value.reshape(*before, size, -1, *after), dim, 0)
+
+
+def laid_out(blocks, dim):
+    blocks = jnp.moveaxis(blocks, 0, dim)
+    lengths = blocks.shape
+    return blocks.reshape(*lengths[:dim], lengths[dim] * lengths[dim + 1], *lengths[dim + 2 :])
+
+
+def exchange_directly(x, axis, split_dim, concat_dim):
+    peers, index = (lax.axis_size(axis), lax.axis_index(axis))
+    blocks = split_up(x, split_dim, peers)
+    finished = [blocks[index]]
+    for lap in range(1, peers):
+        sent = blocks[(index + lap) % peers]
+        finished.append(lax.ppermute(sent, axis, [(i, (i + lap) % peers) for i in range(peers)]))
+    blocks = jnp.stack(finished)[(index - jnp.arange(peers)) % peers]
+    return laid_out(blocks, concat_dim)
 
 
 def padded(cells, sides, width):
@@ -58,7 +80,7 @@
     moved = (
         lax.all_to_all(query, "head", split_axis=2, concat_axis=1, tiled=True),
         lax.all_to_all(key, "head", split_axis=2, concat_axis=1, tiled=True),
-        lax.all_to_all(value, "head", split_axis=2, concat_axis=1, tiled=True),
+        exchange_directly(value, "head", 2, 1),
         lax.all_to_all(resid_in, "head", split_axis=2, concat_axis=1, tiled=True),
         lax.all_to_all(out_grad, "head", split_axis=2, concat_axis=1, tiled=True),
     )

time: 207 us -> 200 us (0.966)
  local copies, waits for them, and re-layouts: 39.1 us -> 29.7 us
  matrix products: 34.8 us -> 38.2 us
    ppermute x8 -> x4, local copies, waits for them, and re-layouts: 12 us -> 5.39 us  [shifted(): lax.ppermute(value, axis, [(source, source + steps) for source in range(f...]
    all_to_all x1 -> x0, starting transfers between devices: 4.96 us -> none  [on_device(): lax.all_to_all(value, 'head', split_axis=2, concat_axis=1, tiled=True)]
    dot_general x5, matrix products: 3 us -> 7.07 us  [block_slopes(): jnp.einsum('qhd,khd->hqk', grad_heads, values_now, preferred_element_type...]
    unnamed x90 -> x77, local copies, waits for them, and re-layouts: 13.2 us -> 10.2 us
    ppermute x0 -> x3, starting transfers between devices: none -> 2.16 us  [exchange_directly(): lax.ppermute(sent, axis, [(i, (i + lap) % peers) for i in range(peers)])]
    unnamed x5 -> x4, other arithmetic: 8.65 us -> 7.24 us
  transfers between devices with their start and end apart: 26 -> 28, of which waited for: 2 -> 2; matrix products, arithmetic and copies ran while one was open for 27% -> 29% of each run, Pallas kernels for 0% -> 0%
where the time goes in v1:
time: 200 us; the launch traced here: 198 us
  starting transfers between devices  83.8 us (42%)
  matrix products  38.2 us (19%)
  local copies, waits for them, and re-layouts  29.7 us (15%)
  other arithmetic  25.3 us (13%)
  between operations  15.1 us (8%)
  waiting for transfers between devices  5.89 us (3%)
    ppermute x16, starting transfers between devices, shifted(): lax.ppermute(value, axis, [(source, source + steps) for source in range(f...  51.5 us
    dot_general x5, matrix products, block_logits(): jnp.einsum('qhd,khd->hqk', query_heads, keys_now, preferred_element_type=...  12.6 us
    unnamed x77, local copies, waits for them, and re-layouts  10.2 us
    ppermute x2, starting transfers between devices, padded(): lax.ppermute(tail, axis, [(i, (i + 1) % count) for i in range(ends)])  9.64 us
    dot_general x5, matrix products, on_device(): jnp.einsum('hqk,qhd->khd', dlogits, query_heads, preferred_element_type=j...  7.3 us
    unnamed x4, other arithmetic  7.24 us
    dot_general x5, matrix products, block_slopes(): jnp.einsum('qhd,khd->hqk', grad_heads, values_now, preferred_element_type...  7.07 us
    reshape x4, local copies, waits for them, and re-layouts, on_device(): key_part = (jnp.einsum('hqk,qhd->khd', dlogits, query_heads, preferred_el...  6.71 us
  transfers between devices with their start and end apart: 28, of which 2 were waited for; matrix products, arithmetic and copies ran while one was open for 29% of the time, Pallas kernels for 0%

profile of v1, /device:TPU:14, one launch (start us, length us, event | category | flops | bytes accessed | tf_op | source)
XLA Modules:
  0.0 198.1 jit_solution(363165584705593885)
XLA Ops:
  7.2 1.1 copy.212
  9.4 1.5 collective-permute-start.10
  12.5 1.4 reduce.3
  14.6 4.8 %all-to-all-start.2 = ((bf16[4,2,8192]{2,1,0:T(2,128)(2,1)}), bf16[4,2,8192]{2,1,0:T(2,128)(2,1)S(1)}, u32[]{:S(2)}, u32[]{:S(2)}) async-start(bf16[4,2,8192]{2,1,0:T(2,128)(2,1)} %reshape.575), calls=%async_computation.2 | async-start | bytes 262144 | tf_op jit(solution)/shard_map/all_to_all | solution.py:81
  21.5 1.3 iota_compare_fusion.2
  22.8 1.3 iota_compare_fusion
  24.1 3.0 %fusion.33 = (pred[512,512]{0,1:T(8,128)(4,1)}, pred[512,512]{0,1:T(8,128)(4,1)}, pred[512,512]{0,1:T(8,128)(4,1)}, pred[512,512]{0,1:T(8,128)(4,1)}, pred[512,512]{0,1:T(8,128)(4,1)}) fusion(s32[512]{0:T(512)S(1)} %get-tuple-element.120, s32[512]{0:T(512)S(1)} %iota_add_fusion.4, pred[512]{0:T(512)(128)(4,1)S(1)} %get-tuple-element.118, pred[]{:T(512)S(6)} %and.200, ...), kind=kLoop, calls=%fused_computation.73 | loop fusion | flops 6553600 | bytes 1323525 | tf_op jit(solution)/shard_map/and | solution.py:132
  27.3 1.4 reduce.2
  29.8 2.2 %reduce.1 = bf16[1024,128]{1,0:T(8,128)(2,1)S(1)} reduce(bf16[1024,1,128]{2,1,0:T(2,128)(2,1)S(1)} %bitcast.185, bf16[]{:T(256)} %broadcast.351), dimensions={1}, to_apply=%bitcast.120.reduce_sub_computation | reduce | bytes 524290
  32.8 3.4 %all-to-all-start.3 = ((bf16[4,2,8192]{2,1,0:T(2,128)(2,1)}), bf16[4,2,8192]{2,1,0:T(2,128)(2,1)S(1)}, u32[]{:S(2)}, u32[]{:S(2)}) async-start(bf16[4,2,8192]{2,1,0:T(2,128)(2,1)} %reshape.573), calls=%async_computation.3 | async-start | bytes 262144 | tf_op jit(solution)/shard_map/all_to_all | solution.py:82
  36.2 3.0 %all-to-all-done.3 = bf16[4,2,8192]{2,1,0:T(2,128)(2,1)S(1)} async-done(((bf16[4,2,8192]{2,1,0:T(2,128)(2,1)}), bf16[4,2,8192]{2,1,0:T(2,128)(2,1)S(1)}, u32[]{:S(2)}, u32[]{:S(2)}) %all-to-all-start.3) | async-done | bytes 131104 | tf_op jit(solution)/shard_map/all_to_all | solution.py:82
  39.1 5.0 %all-to-all-start.1 = ((bf16[4,2,16384]{2,1,0:T(2,128)(2,1)}), bf16[4,2,16384]{2,1,0:T(2,128)(2,1)S(1)}, u32[]{:S(2)}, u32[]{:S(2)}) async-start(bf16[4,2,16384]{2,1,0:T(2,128)(2,1)} %reshape.571), calls=%async_computation.1 | async-start | bytes 524288 | tf_op jit(solution)/shard_map/all_to_all | solution.py:84
  44.7 2.2 %reduce = bf16[1024,128]{1,0:T(8,128)(2,1)S(1)} reduce(bf16[1024,1,128]{2,1,0:T(2,128)(2,1)S(1)} %bitcast.184, bf16[]{:T(256)} %broadcast.351), dimensions={1}, to_apply=%bitcast.118.reduce_sub_computation | reduce | bytes 524290
  49.2 2.4 %collective-permute-start.13 = (bf16[512,128]{0,1:T(8,128)(2,1)}, bf16[512,128]{0,1:T(8,128)(2,1)}, u32[]{:S(2)}, u32[]{:S(2)}) collective-permute-start(bf16[512,128]{0,1:T(8,128)(2,1)} %copy.219), channel_id=1, source_target_pairs={{1,0},{2,1},{3,2},{4,3},{5,4},{6,5},{7,6},{9,8},{10,9},{11,10},{12... | collective-permute-start | bytes 393224 | tf_op jit(solution)/shard_map/ppermute | solution.py:53
  51.6 4.3 %collective-permute-start.11 = (bf16[512,128]{0,1:T(8,128)(2,1)}, bf16[512,128]{0,1:T(8,128)(2,1)}, u32[]{:S(2)}, u32[]{:S(2)}) collective-permute-start(bf16[512,128]{0,1:T(8,128)(2,1)} %copy.219), channel_id=1, source_target_pairs={{0,1},{1,2},{2,3},{3,4},{4,5},{5,6},{6,7},{8,9},{9,10},{10,11},{11... | collective-permute-start | bytes 393224 | tf_op jit(solution)/shard_map/ppermute | solution.py:53
  57.5 1.9 collective-permute-start.6
  59.4 3.4 %all-to-all-start = ((bf16[4,2,16384]{2,1,0:T(2,128)(2,1)}), bf16[4,2,16384]{2,1,0:T(2,128)(2,1)S(1)}, u32[]{:S(2)}, u32[]{:S(2)}) async-start(bf16[4,2,16384]{2,1,0:T(2,128)(2,1)} %reshape.569), calls=%async_computation | async-start | bytes 524288 | tf_op jit(solution)/shard_map/all_to_all | solution.py:85
  63.4 4.8 %collective-permute-start.2 = (bf16[30,256]{1,0:T(8,128)(2,1)S(1)}, bf16[30,256]{1,0:T(8,128)(2,1)S(1)}, u32[]{:S(2)}, u32[]{:S(2)}) collective-permute-start(bf16[30,256]{1,0:T(8,128)(2,1)S(1)} %get-tuple-element.44), channel_id=1, source_target_pairs={{0,1},{1,2},{2,3},{3,4},{4,5},{5,6},{6,7},{8,9},{9,10},{10,11},{11... | collective-permute-start | bytes 46088 | tf_op jit(solution)/shard_map/ppermute | solution.py:41
  68.2 1.9 collective-permute-start.3
  70.6 4.8 %collective-permute-start = (bf16[30,256]{1,0:T(8,128)(2,1)S(1)}, bf16[30,256]{1,0:T(8,128)(2,1)S(1)}, u32[]{:S(2)}, u32[]{:S(2)}) collective-permute-start(bf16[30,256]{1,0:T(8,128)(2,1)S(1)} %get-tuple-element.46), channel_id=1, source_target_pairs={{0,1},{1,2},{2,3},{3,4},{4,5},{5,6},{6,7},{8,9},{9,10},{10,11},{11... | collective-permute-start | bytes 46088 | tf_op jit(solution)/shard_map/ppermute | solution.py:41
  75.5 1.9 collective-permute-start.1
  77.5 5.0 %collective-permute-start.4 = (bf16[512,128]{1,0:T(8,128)(2,1)}, bf16[512,128]{1,0:T(8,128)(2,1)}, u32[]{:S(2)}, u32[]{:S(2)}) collective-permute-start(bf16[512,128]{1,0:T(8,128)(2,1)} %bitcast.40), channel_id=1, source_target_pairs={{0,1},{1,2},{2,3},{3,4},{4,5},{5,6},{6,7},{8,9},{9,10},{10,11},{11... | collective-permute-start | bytes 393224 | tf_op jit(solution)/shard_map/ppermute | solution.py:53
  82.6 2.4 %slice_multiply_fusion.31 = f32[542,256]{1,0:T(8,128)S(1)} fusion(f32[572,256]{1,0:T(8,128)S(1)} %maximum_convert_fusion, f32[572,256]{1,0:T(8,128)S(1)} %maximum_convert_fusion.1, f32[256]{0:T(256)S(1)} %bitcast.229, f32[256]{0:T(256)S(1)} %bitcast.231, f32[256]{0:T(256)S(1)} %bitcast.233, f32[256]{0:T(256)S(1)} %bitcast.235, f32[256]{0:T(256)S(1)} %bitcast.237, ...), kind=kLoop, calls=%fused_computation.141 | loop fusion | flops 9573888 | bytes 18347008 | tf_op jit(solution)/shard_map/mul | solution.py:68
  85.0 2.8 %fusion.71 = bf16[512,256]{1,0:T(8,128)(2,1)} fusion(f32[542,256]{1,0:T(8,128)S(1)} %slice_multiply_fusion.31, f32[572,256]{1,0:T(8,128)S(1)} %maximum_convert_fusion, f32[256]{0:T(256)S(1)} %bitcast.230, f32[256]{0:T(256)S(1)} %bitcast.232, f32[256]{0:T(256)S(1)} %bitcast.234, f32[256]{0:T(256)S(1)} %bitcast.236, f32[256]{0:T(256)S(1)} %bitcast.238, ...), kind=kLoop, calls=%fused_computation.144 | loop fusion | flops 8257536 | bytes 17071104 | tf_op jit(solution)/shard_map/convert_element_type | solution.py:73
  87.9 1.6 fusion.117
  89.4 1.9 collective-permute-start.14
  91.4 4.8 %collective-permute-start.12 = (bf16[512,128]{0,1:T(8,128)(2,1)}, bf16[512,128]{0,1:T(8,128)(2,1)}, u32[]{:S(2)}, u32[]{:S(2)}) collective-permute-start(bf16[512,128]{0,1:T(8,128)(2,1)} %collective-permute-done.11), channel_id=1, source_target_pairs={{0,1},{1,2},{2,3},{3,4},{4,5},{5,6},{6,7},{8,9},{9,10},{10,11},{11... | collective-permute-start | bytes 393224 | tf_op jit(solution)/shard_map/ppermute | solution.py:53
  97.3 1.9 collective-permute-start.7
  99.2 1.7 copy.209
  100.9 4.9 %collective-permute-start.5 = (bf16[512,128]{1,0:T(8,128)(2,1)}, bf16[512,128]{1,0:T(8,128)(2,1)}, u32[]{:S(2)}, u32[]{:S(2)}) collective-permute-start(bf16[512,128]{1,0:T(8,128)(2,1)} %collective-permute-done.4), channel_id=1, source_target_pairs={{0,1},{1,2},{2,3},{3,4},{4,5},{5,6},{6,7},{8,9},{9,10},{10,11},{11... | collective-permute-start | bytes 393224 | tf_op jit(solution)/shard_map/ppermute | solution.py:53
  105.8 3.5 %fusion.115 = (f32[2,512]{1,0:T(2,128)}, f32[2,512,512]{1,2,0:T(8,128)}) fusion(bf16[512,2,64]{0,2,1:T(8,128)(2,1)S(1)} %reshape_squeeze.8, bf16[512,2,64]{0,2,1:T(8,128)(2,1)S(1)} %bitcast.215, pred[512,512]{0,1:T(8,128)(4,1)} %get-tuple-element.90), kind=kOutput, calls=%fused_computation.250 | convolution fusion | flops 68680704 | bytes 2625536 | tf_op jit(solution)/shard_map/qhd,khd->hqk/dot_general | solution.py:147
  109.3 2.5 %fusion.116 = (f32[2,512]{1,0:T(2,128)}, f32[2,512,512]{1,2,0:T(8,128)}) fusion(bf16[512,2,64]{0,2,1:T(8,128)(2,1)S(1)} %reshape_squeeze.8, bf16[512,2,64]{0,2,1:T(8,128)(2,1)S(1)} %bitcast.219, pred[512,512]{0,1:T(8,128)(4,1)S(1)} %copy-done.22), kind=kOutput, calls=%fused_computation.251 | convolution fusion | flops 68680704 | bytes 2625536 | tf_op jit(solution)/shard_map/qhd,khd->hqk/dot_general | solution.py:147
  112.9 1.7 copy.208
  114.6 3.0 %fusion.118 = (f32[2,512]{1,0:T(2,128)S(1)}, f32[2,512,512]{1,2,0:T(8,128)}) fusion(bf16[512,2,64]{0,2,1:T(8,128)(2,1)S(1)} %reshape_squeeze.8, bf16[512,2,64]{0,2,1:T(8,128)(2,1)} %bitcast.217, pred[512,512]{0,1:T(8,128)(4,1)} %get-tuple-element.88), kind=kOutput, calls=%fused_computation.253 | convolution fusion | flops 68680704 | bytes 2625536 | tf_op jit(solution)/shard_map/qhd,khd->hqk/dot_general | solution.py:147
  117.6 2.0 %fusion.114 = (f32[2,512]{1,0:T(2,128)S(1)}, f32[2,512,512]{1,2,0:T(8,128)}) fusion(bf16[512,2,64]{0,2,1:T(8,128)(2,1)S(1)} %reshape_squeeze.8, bf16[512,2,64]{0,2,1:T(8,128)(2,1)S(1)} %bitcast.202, pred[512,512]{0,1:T(8,128)(4,1)S(1)} %copy-done.21), kind=kOutput, calls=%fused_computation.249 | convolution fusion | flops 68680704 | bytes 2625536 | tf_op jit(solution)/shard_map/qhd,khd->hqk/dot_general | solution.py:147
  119.7 1.7 convolution_convert_fusion.5
  123.0 1.7 multiply_reduce_fusion
  124.7 1.7 multiply_reduce_fusion.1
  126.4 1.7 multiply_reduce_fusion.2
  128.1 1.5 multiply_reduce_fusion.3
  130.5 1.1 convolution_convert_fusion.1
  131.7 1.1 convolution_convert_fusion
  132.8 1.2 fusion.12
  134.0 4.2 %multiply_convert_fusion = (bf16[2,512,512]{1,2,0:T(8,128)(2,1)}, bf16[2,512,512]{1,2,0:T(8,128)(2,1)}, bf16[2,512,512]{1,2,0:T(8,128)(2,1)}, bf16[2,512,512]{1,2,0:T(8,128)(2,1)S(1)}, bf16[2,512,512]{1,2,0:T(8,128)(2,1)}) fusion(f32[2,512,512]{1,2,0:T(8,128)S(1)} %get-tuple-element.108, f32[2,512,512]{1,2,0:T(8,128)S(1)} %copy-done.4, ...), kind=kLoop, calls=%fused_computation.1 | loop fusion | flops 10485760 | bytes 26222592 | tf_op jit(solution)/shard_map/convert_element_type | solution.py:181
  138.3 1.1 fusion.17
  143.6 1.1 fusion.18
  144.7 1.7 copy.235
  146.5 2.3 %fusion.15 = bf16[2,512,64]{1,2,0:T(8,128)(2,1)} fusion(bf16[2,512,512]{1,2,0:T(8,128)(2,1)} %get-tuple-element.84, bf16[512,2,64]{0,2,1:T(8,128)(2,1)S(1)} %reshape_squeeze.8), kind=kOutput, calls=%fused_computation.55 | convolution fusion | flops 67239936 | bytes 1310720 | tf_op jit(solution)/shard_map/hqk,qhd->khd/dot_general | solution.py:190
  148.8 1.7 copy.228
  150.4 2.3 %fusion.16 = bf16[2,512,64]{1,2,0:T(8,128)(2,1)} fusion(bf16[2,512,512]{1,2,0:T(8,128)(2,1)} %get-tuple-element.85, bf16[512,2,64]{0,2,1:T(8,128)(2,1)S(1)} %reshape_squeeze.8), kind=kOutput, calls=%fused_computation.56 | convolution fusion | flops 67239936 | bytes 1310720 | tf_op jit(solution)/shard_map/hqk,qhd->khd/dot_general | solution.py:190
  152.8 1.6 copy.231
  154.4 1.7 copy.233
  156.1 1.3 fusion.119
  157.4 1.6 convolution_add_fusion.2
  160.3 1.7 copy.246
  162.0 2.0 %collective-permute-start.17 = (bf16[512,128]{1,0:T(8,128)(2,1)}, bf16[512,128]{1,0:T(8,128)(2,1)S(1)}, u32[]{:S(2)}, u32[]{:S(2)}) collective-permute-start(bf16[512,128]{1,0:T(8,128)(2,1)} %copy.233), channel_id=1, source_target_pairs={{0,1},{1,2},{2,3},{3,4},{4,5},{5,6},{6,7},{8,9},{9,10},{10,11},{11... | collective-permute-start | bytes 393224 | tf_op jit(solution)/shard_map/ppermute | solution.py:53
  164.0 3.8 %collective-permute-start.16 = (bf16[512,128]{1,0:T(8,128)(2,1)}, bf16[512,128]{1,0:T(8,128)(2,1)S(1)}, u32[]{:S(2)}, u32[]{:S(2)}) collective-permute-start(bf16[512,128]{1,0:T(8,128)(2,1)} %copy.231), channel_id=1, source_target_pairs={{1,0},{2,1},{3,2},{4,3},{5,4},{6,5},{7,6},{9,8},{10,9},{11,10},{12... | collective-permute-start | bytes 393224 | tf_op jit(solution)/shard_map/ppermute | solution.py:53
  167.8 2.4 %collective-permute-start.15 = (bf16[512,128]{1,0:T(8,128)(2,1)}, bf16[512,128]{1,0:T(8,128)(2,1)S(1)}, u32[]{:S(2)}, u32[]{:S(2)}) collective-permute-start(bf16[512,128]{1,0:T(8,128)(2,1)} %copy.228), channel_id=1, source_target_pairs={{2,0},{3,1},{4,2},{5,3},{6,4},{7,5},{10,8},{11,9},{12,10},{13,11},... | collective-permute-start | bytes 393224 | tf_op jit(solution)/shard_map/ppermute | solution.py:53
  170.2 3.5 %collective-permute-start.18 = (bf16[512,128]{1,0:T(8,128)(2,1)}, bf16[512,128]{1,0:T(8,128)(2,1)S(1)}, u32[]{:S(2)}, u32[]{:S(2)}) collective-permute-start(bf16[512,128]{1,0:T(8,128)(2,1)} %copy.235), channel_id=1, source_target_pairs={{0,2},{1,3},{2,4},{3,5},{4,6},{5,7},{8,10},{9,11},{10,12},{11,13},... | collective-permute-start | bytes 393224 | tf_op jit(solution)/shard_map/ppermute | solution.py:53
  174.3 2.4 %collective-permute-start.19 = (bf16[512,128]{1,0:T(8,128)(2,1)}, bf16[512,128]{1,0:T(8,128)(2,1)S(1)}, u32[]{:S(2)}, u32[]{:S(2)}) collective-permute-start(bf16[512,128]{1,0:T(8,128)(2,1)} %copy.238), channel_id=1, source_target_pairs={{2,0},{3,1},{4,2},{5,3},{6,4},{7,5},{10,8},{11,9},{12,10},{13,11},... | collective-permute-start | bytes 393224 | tf_op jit(solution)/shard_map/ppermute | solution.py:53
  176.7 1.9 collective-permute-start.20
  178.6 4.8 %collective-permute-start.21 = (bf16[512,128]{1,0:T(8,128)(2,1)}, bf16[512,128]{1,0:T(8,128)(2,1)S(1)}, u32[]{:S(2)}, u32[]{:S(2)}) collective-permute-start(bf16[512,128]{1,0:T(8,128)(2,1)} %copy.243), channel_id=1, source_target_pairs={{0,1},{1,2},{2,3},{3,4},{4,5},{5,6},{6,7},{8,9},{9,10},{10,11},{11... | collective-permute-start | bytes 393224 | tf_op jit(solution)/shard_map/ppermute | solution.py:53
  183.5 3.5 %collective-permute-start.22 = (bf16[512,128]{1,0:T(8,128)(2,1)}, bf16[512,128]{1,0:T(8,128)(2,1)S(1)}, u32[]{:S(2)}, u32[]{:S(2)}) collective-permute-start(bf16[512,128]{1,0:T(8,128)(2,1)} %copy.245), channel_id=1, source_target_pairs={{0,2},{1,3},{2,4},{3,5},{4,6},{5,7},{8,10},{9,11},{10,12},{11,13},... | collective-permute-start | bytes 393224 | tf_op jit(solution)/shard_map/ppermute | solution.py:53
  187.7 2.8 %collective-permute-done.22 = bf16[512,128]{1,0:T(8,128)(2,1)S(1)} collective-permute-done((bf16[512,128]{1,0:T(8,128)(2,1)}, bf16[512,128]{1,0:T(8,128)(2,1)S(1)}, u32[]{:S(2)}, u32[]{:S(2)}) %collective-permute-start.22) | collective-permute-done | bytes 131104 | tf_op jit(solution)/shard_map/ppermute | solution.py:53
  (156 shorter events, 25.0 us)
Async XLA Ops:
  7.2 112.5 %copy-start = (bf16[512,1024]{1,0:T(8,128)(2,1)S(1)}, bf16[512,1024]{1,0:T(8,128)(2,1)}, u32[]{:S(2)}) copy-start(bf16[512,1024]{1,0:T(8,128)(2,1)} %param.13) | copy-start | bytes 3145732
  7.2 12.2 %copy-start.26 = (s32[8]{0:T(128)S(1)}, s32[8]{0:T(128)}, u32[]{:S(2)}) copy-start(s32[8]{0:T(128)} %param.15) | copy-start | bytes 100
  7.2 19.9 %copy-start.23 = (bf16[1,128,512]{2,1,0:T(8,128)(2,1)S(1)}, bf16[1,128,512]{2,1,0:T(8,128)(2,1)}, u32[]{:S(2)}) copy-start(bf16[1,128,512]{2,1,0:T(8,128)(2,1)} %param.9) | copy-start | bytes 393220
  8.4 21.0 %copy-start.19 = (bf16[1,128,1024]{2,1,0:T(8,128)(2,1)S(1)}, bf16[1,128,1024]{2,1,0:T(8,128)(2,1)}, u32[]{:S(2)}) copy-start(bf16[1,128,1024]{2,1,0:T(8,128)(2,1)} %param.11) | copy-start | bytes 786436
  8.5 39.1 %collective-permute-start.8 = (bf16[1,128,128]{2,1,0:T(8,128)(2,1)S(1)}, bf16[1,128,128]{2,1,0:T(8,128)(2,1)S(1)}, u32[]{:S(2)}, u32[]{:S(2)}) collective-permute-start(bf16[1,128,128]{2,1,0:T(8,128)(2,1)S(1)} %bitcast.221), channel_id=1, source_target_pairs={{0,8},{8,16},{16,24},{24,0},{1,9},{9,17},{17,25},{25,1},{2,10},{10... | collective-permute-start | bytes 98312 | tf_op jit(solution)/shard_map/ppermute | solution.py:28
  8.7 39.0 %collective-permute-start.9 = (bf16[1,128,128]{2,1,0:T(8,128)(2,1)S(1)}, bf16[1,128,128]{2,1,0:T(8,128)(2,1)S(1)}, u32[]{:S(2)}, u32[]{:S(2)}) collective-permute-start(bf16[1,128,128]{2,1,0:T(8,128)(2,1)S(1)} %bitcast.222), channel_id=1, source_target_pairs={{0,16},{8,24},{16,0},{24,8},{1,17},{9,25},{17,1},{25,9},{2,18},{10... | collective-permute-start | bytes 98312 | tf_op jit(solution)/shard_map/ppermute | solution.py:28
  9.4 38.3 %collective-permute-start.10 = (bf16[1,128,128]{2,1,0:T(8,128)(2,1)S(1)}, bf16[1,128,128]{2,1,0:T(8,128)(2,1)S(1)}, u32[]{:S(2)}, u32[]{:S(2)}) collective-permute-start(bf16[1,128,128]{2,1,0:T(8,128)(2,1)S(1)} %bitcast.223), channel_id=1, source_target_pairs={{0,24},{8,0},{16,8},{24,16},{1,25},{9,1},{17,9},{25,17},{2,26},{10... | collective-permute-start | bytes 98312 | tf_op jit(solution)/shard_map/ppermute | solution.py:28
  14.6 18.1 %all-to-all-start.2 = ((bf16[4,2,8192]{2,1,0:T(2,128)(2,1)}), bf16[4,2,8192]{2,1,0:T(2,128)(2,1)S(1)}, u32[]{:S(2)}, u32[]{:S(2)}) async-start(bf16[4,2,8192]{2,1,0:T(2,128)(2,1)} %reshape.575), calls=%async_computation.2 | async-start | bytes 262144 | tf_op jit(solution)/shard_map/all_to_all | solution.py:81
  27.1 17.2 %copy-start.20 = (bf16[1,128,1024]{2,1,0:T(8,128)(2,1)S(1)}, bf16[1,128,1024]{2,1,0:T(8,128)(2,1)}, u32[]{:S(2)}) copy-start(bf16[1,128,1024]{2,1,0:T(8,128)(2,1)} %param.12) | copy-start | bytes 786436
  32.8 6.3 %all-to-all-start.3 = ((bf16[4,2,8192]{2,1,0:T(2,128)(2,1)}), bf16[4,2,8192]{2,1,0:T(2,128)(2,1)S(1)}, u32[]{:S(2)}, u32[]{:S(2)}) async-start(bf16[4,2,8192]{2,1,0:T(2,128)(2,1)} %reshape.573), calls=%async_computation.3 | async-start | bytes 262144 | tf_op jit(solution)/shard_map/all_to_all | solution.py:82
  39.1 20.3 %all-to-all-start.1 = ((bf16[4,2,16384]{2,1,0:T(2,128)(2,1)}), bf16[4,2,16384]{2,1,0:T(2,128)(2,1)S(1)}, u32[]{:S(2)}, u32[]{:S(2)}) async-start(bf16[4,2,16384]{2,1,0:T(2,128)(2,1)} %reshape.571), calls=%async_computation.1 | async-start | bytes 524288 | tf_op jit(solution)/shard_map/all_to_all | solution.py:84
  49.2 40.2 %collective-permute-start.13 = (bf16[512,128]{0,1:T(8,128)(2,1)}, bf16[512,128]{0,1:T(8,128)(2,1)}, u32[]{:S(2)}, u32[]{:S(2)}) collective-permute-start(bf16[512,128]{0,1:T(8,128)(2,1)} %copy.219), channel_id=1, source_target_pairs={{1,0},{2,1},{3,2},{4,3},{5,4},{6,5},{7,6},{9,8},{10,9},{11,10},{12... | collective-permute-start | bytes 393224 | tf_op jit(solution)/shard_map/ppermute | solution.py:53
  51.6 39.8 %collective-permute-start.11 = (bf16[512,128]{0,1:T(8,128)(2,1)}, bf16[512,128]{0,1:T(8,128)(2,1)}, u32[]{:S(2)}, u32[]{:S(2)}) collective-permute-start(bf16[512,128]{0,1:T(8,128)(2,1)} %copy.219), channel_id=1, source_target_pairs={{0,1},{1,2},{2,3},{3,4},{4,5},{5,6},{6,7},{8,9},{9,10},{10,11},{11... | collective-permute-start | bytes 393224 | tf_op jit(solution)/shard_map/ppermute | solution.py:53
  57.4 30.4 %copy-start.14 = (bf16[512,2,64]{0,2,1:T(8,128)(2,1)}, bf16[512,2,64]{0,2,1:T(8,128)(2,1)S(1)}, u32[]{:S(2)}) copy-start(bf16[512,2,64]{0,2,1:T(8,128)(2,1)S(1)} %reshape_squeeze.9) | copy-start | bytes 393220
  57.5 38.8 %collective-permute-start.6 = (bf16[512,128]{1,0:T(8,128)(2,1)}, bf16[512,128]{1,0:T(8,128)(2,1)}, u32[]{:S(2)}, u32[]{:S(2)}) collective-permute-start(bf16[512,128]{1,0:T(8,128)(2,1)} %bitcast.40), channel_id=1, source_target_pairs={{1,0},{2,1},{3,2},{4,3},{5,4},{6,5},{7,6},{9,8},{10,9},{11,10},{12... | collective-permute-start | bytes 393224 | tf_op jit(solution)/shard_map/ppermute | solution.py:53
  59.4 10.7 %all-to-all-start = ((bf16[4,2,16384]{2,1,0:T(2,128)(2,1)}), bf16[4,2,16384]{2,1,0:T(2,128)(2,1)S(1)}, u32[]{:S(2)}, u32[]{:S(2)}) async-start(bf16[4,2,16384]{2,1,0:T(2,128)(2,1)} %reshape.569), calls=%async_computation | async-start | bytes 524288 | tf_op jit(solution)/shard_map/all_to_all | solution.py:85
  62.8 56.9 %all-gather.2.cloned.1.call-start = ((), (), s32[]{:S(2)}) async-start(), calls=%async_computation.4 | async-start | bytes 1310720 | tf_op jit(solution)/shard_map/all_gather | solution.py:107
  63.4 7.3 %collective-permute-start.2 = (bf16[30,256]{1,0:T(8,128)(2,1)S(1)}, bf16[30,256]{1,0:T(8,128)(2,1)S(1)}, u32[]{:S(2)}, u32[]{:S(2)}) collective-permute-start(bf16[30,256]{1,0:T(8,128)(2,1)S(1)} %get-tuple-element.44), channel_id=1, source_target_pairs={{0,1},{1,2},{2,3},{3,4},{4,5},{5,6},{6,7},{8,9},{9,10},{10,11},{11... | collective-permute-start | bytes 46088 | tf_op jit(solution)/shard_map/ppermute | solution.py:41
  68.2 7.3 %collective-permute-start.3 = (bf16[30,256]{1,0:T(8,128)(2,1)S(1)}, bf16[30,256]{1,0:T(8,128)(2,1)S(1)}, u32[]{:S(2)}, u32[]{:S(2)}) collective-permute-start(bf16[30,256]{1,0:T(8,128)(2,1)S(1)} %get-tuple-element.45), channel_id=1, source_target_pairs={{1,0},{2,1},{3,2},{4,3},{5,4},{6,5},{7,6},{9,8},{10,9},{11,10},{12... | collective-permute-start | bytes 46088 | tf_op jit(solution)/shard_map/ppermute | solution.py:43
  70.6 6.8 %collective-permute-start = (bf16[30,256]{1,0:T(8,128)(2,1)S(1)}, bf16[30,256]{1,0:T(8,128)(2,1)S(1)}, u32[]{:S(2)}, u32[]{:S(2)}) collective-permute-start(bf16[30,256]{1,0:T(8,128)(2,1)S(1)} %get-tuple-element.46), channel_id=1, source_target_pairs={{0,1},{1,2},{2,3},{3,4},{4,5},{5,6},{6,7},{8,9},{9,10},{10,11},{11... | collective-permute-start | bytes 46088 | tf_op jit(solution)/shard_map/ppermute | solution.py:41
  75.5 7.0 %collective-permute-start.1 = (bf16[30,256]{1,0:T(8,128)(2,1)S(1)}, bf16[30,256]{1,0:T(8,128)(2,1)S(1)}, u32[]{:S(2)}, u32[]{:S(2)}) collective-permute-start(bf16[30,256]{1,0:T(8,128)(2,1)S(1)} %get-tuple-element.47), channel_id=1, source_target_pairs={{1,0},{2,1},{3,2},{4,3},{5,4},{6,5},{7,6},{9,8},{10,9},{11,10},{12... | collective-permute-start | bytes 46088 | tf_op jit(solution)/shard_map/ppermute | solution.py:43
  77.5 21.7 %collective-permute-start.4 = (bf16[512,128]{1,0:T(8,128)(2,1)}, bf16[512,128]{1,0:T(8,128)(2,1)}, u32[]{:S(2)}, u32[]{:S(2)}) collective-permute-start(bf16[512,128]{1,0:T(8,128)(2,1)} %bitcast.40), channel_id=1, source_target_pairs={{0,1},{1,2},{2,3},{3,4},{4,5},{5,6},{6,7},{8,9},{9,10},{10,11},{11... | collective-permute-start | bytes 393224 | tf_op jit(solution)/shard_map/ppermute | solution.py:53
  89.4 32.6 %collective-permute-start.14 = (bf16[512,128]{0,1:T(8,128)(2,1)}, bf16[512,128]{0,1:T(8,128)(2,1)}, u32[]{:S(2)}, u32[]{:S(2)}) collective-permute-start(bf16[512,128]{0,1:T(8,128)(2,1)} %collective-permute-done.13), channel_id=1, source_target_pairs={{1,0},{2,1},{3,2},{4,3},{5,4},{6,5},{7,6},{9,8},{10,9},{11,10},{12... | collective-permute-start | bytes 393224 | tf_op jit(solution)/shard_map/ppermute | solution.py:53
  91.4 36.7 %collective-permute-start.12 = (bf16[512,128]{0,1:T(8,128)(2,1)}, bf16[512,128]{0,1:T(8,128)(2,1)}, u32[]{:S(2)}, u32[]{:S(2)}) collective-permute-start(bf16[512,128]{0,1:T(8,128)(2,1)} %collective-permute-done.11), channel_id=1, source_target_pairs={{0,1},{1,2},{2,3},{3,4},{4,5},{5,6},{6,7},{8,9},{9,10},{10,11},{11... | collective-permute-start | bytes 393224 | tf_op jit(solution)/shard_map/ppermute | solution.py:53
  97.2 14.6 %copy-start.15 = (bf16[512,128]{0,1:T(8,128)(2,1)}, bf16[512,128]{0,1:T(8,128)(2,1)S(1)}, u32[]{:S(2)}) copy-start(bf16[512,128]{0,1:T(8,128)(2,1)S(1)} %copy.210) | copy-start | bytes 393220
  97.3 14.6 %collective-permute-start.7 = (bf16[512,128]{1,0:T(8,128)(2,1)}, bf16[512,128]{1,0:T(8,128)(2,1)}, u32[]{:S(2)}, u32[]{:S(2)}) collective-permute-start(bf16[512,128]{1,0:T(8,128)(2,1)} %collective-permute-done.6), channel_id=1, source_target_pairs={{1,0},{2,1},{3,2},{4,3},{5,4},{6,5},{7,6},{9,8},{10,9},{11,10},{12... | collective-permute-start | bytes 393224 | tf_op jit(solution)/shard_map/ppermute | solution.py:53
  100.9 8.5 %copy-start.17 = (bf16[512,128]{0,1:T(8,128)(2,1)S(1)}, bf16[512,128]{0,1:T(8,128)(2,1)}, u32[]{:S(2)}) copy-start(bf16[512,128]{0,1:T(8,128)(2,1)} %copy.209) | copy-start | bytes 393220
  100.9 8.5 %copy-start.22 = (pred[512,512]{0,1:T(8,128)(4,1)S(1)}, pred[512,512]{0,1:T(8,128)(4,1)}, u32[]{:S(2)}) copy-start(pred[512,512]{0,1:T(8,128)(4,1)} %get-tuple-element.89) | copy-start | bytes 786436
  100.9 12.0 %collective-permute-start.5 = (bf16[512,128]{1,0:T(8,128)(2,1)}, bf16[512,128]{1,0:T(8,128)(2,1)}, u32[]{:S(2)}, u32[]{:S(2)}) collective-permute-start(bf16[512,128]{1,0:T(8,128)(2,1)} %collective-permute-done.4), channel_id=1, source_target_pairs={{0,1},{1,2},{2,3},{3,4},{4,5},{5,6},{6,7},{8,9},{9,10},{10,11},{11... | collective-permute-start | bytes 393224 | tf_op jit(solution)/shard_map/ppermute | solution.py:53
  112.9 6.8 %copy-start.10 = (bf16[512,128]{0,1:T(8,128)(2,1)}, bf16[512,128]{0,1:T(8,128)(2,1)S(1)}, u32[]{:S(2)}) copy-start(bf16[512,128]{0,1:T(8,128)(2,1)S(1)} %copy.211) | copy-start | bytes 393220
  114.6 3.0 %copy-start.21 = (pred[512,512]{0,1:T(8,128)(4,1)S(1)}, pred[512,512]{0,1:T(8,128)(4,1)}, u32[]{:S(2)}) copy-start(pred[512,512]{0,1:T(8,128)(4,1)} %get-tuple-element.91) | copy-start | bytes 786436
  114.6 5.0 %copy-start.27 = (f32[2,512]{1,0:T(2,128)S(1)}, f32[2,512]{1,0:T(2,128)}, u32[]{:S(2)}) copy-start(f32[2,512]{1,0:T(2,128)} %get-tuple-element.100) | copy-start | bytes 12292
  114.6 5.0 %copy-start.28 = (f32[2,512]{1,0:T(2,128)S(1)}, f32[2,512]{1,0:T(2,128)}, u32[]{:S(2)}) copy-start(f32[2,512]{1,0:T(2,128)} %get-tuple-element.102) | copy-start | bytes 12292
  119.7 9.9 %copy-start.24 = (f32[2,512]{1,0:T(2,128)}, f32[2,512]{1,0:T(2,128)S(1)}, u32[]{:S(2)}) copy-start(f32[2,512]{1,0:T(2,128)S(1)} %get-tuple-element.43) | copy-start | bytes 12292
  121.4 1.6 copy-start.4
  123.0 1.7 copy-start.1
  124.7 1.7 copy-start.2
  126.4 1.7 copy-start.3
  131.7 2.3 %copy-start.25 = (f32[2,512]{1,0:T(2,128)S(1)}, f32[2,512]{1,0:T(2,128)}, u32[]{:S(2)}) copy-start(f32[2,512]{1,0:T(2,128)} %copy-done.24) | copy-start | bytes 12292
  134.0 5.4 %copy-start.16 = (bf16[512,128]{0,1:T(8,128)(2,1)S(1)}, bf16[512,128]{0,1:T(8,128)(2,1)}, u32[]{:S(2)}) copy-start(bf16[512,128]{0,1:T(8,128)(2,1)} %copy-done.15) | copy-start | bytes 393220
  138.3 2.2 %copy-start.8 = (f32[2,64,512]{2,1,0:T(8,128)S(1)}, f32[2,64,512]{2,1,0:T(8,128)}, u32[]{:S(2)}) copy-start(f32[2,64,512]{2,1,0:T(8,128)} %fusion.12) | copy-start | bytes 786436
  138.3 2.3 %copy-start.13 = (bf16[2,64,512]{2,1,0:T(8,128)(2,1)S(1)}, bf16[2,64,512]{2,1,0:T(8,128)(2,1)}, u32[]{:S(2)}) copy-start(bf16[2,64,512]{2,1,0:T(8,128)(2,1)} %convolution_convert_fusion) | copy-start | bytes 393220
  138.3 3.1 %copy-start.12 = (bf16[2,64,512]{2,1,0:T(8,128)(2,1)S(1)}, bf16[2,64,512]{2,1,0:T(8,128)(2,1)}, u32[]{:S(2)}) copy-start(bf16[2,64,512]{2,1,0:T(8,128)(2,1)} %convolution_convert_fusion.1) | copy-start | bytes 393220
  138.3 5.4 %copy-start.6 = (bf16[2,512,512]{1,2,0:T(8,128)(2,1)S(1)}, bf16[2,512,512]{1,2,0:T(8,128)(2,1)}, u32[]{:S(2)}) copy-start(bf16[2,512,512]{1,2,0:T(8,128)(2,1)} %get-tuple-element.83) | copy-start | bytes 3145732
  144.7 11.4 %copy-start.5 = (bf16[2,512,512]{1,2,0:T(8,128)(2,1)S(1)}, bf16[2,512,512]{1,2,0:T(8,128)(2,1)}, u32[]{:S(2)}) copy-start(bf16[2,512,512]{1,2,0:T(8,128)(2,1)} %get-tuple-element.87) | copy-start | bytes 3145732
  156.1 3.0 %copy-start.7 = (bf16[2,512,512]{1,2,0:T(8,128)(2,1)S(1)}, bf16[2,512,512]{1,2,0:T(8,128)(2,1)}, u32[]{:S(2)}) copy-start(bf16[2,512,512]{1,2,0:T(8,128)(2,1)} %get-tuple-element.85) | copy-start | bytes 3145732
  156.1 3.0 %copy-start.9 = (f32[2,512,64]{1,2,0:T(8,128)S(1)}, f32[2,512,64]{1,2,0:T(8,128)}, u32[]{:S(2)}) copy-start(f32[2,512,64]{1,2,0:T(8,128)} %fusion.120) | copy-start | bytes 786436
  156.1 3.0 %copy-start.18 = (bf16[512,128]{0,1:T(8,128)(2,1)S(1)}, bf16[512,128]{0,1:T(8,128)(2,1)}, u32[]{:S(2)}) copy-start(bf16[512,128]{0,1:T(8,128)(2,1)} %copy.209) | copy-start | bytes 393220
  157.4 2.0 %copy-start.11 = (bf16[512,128]{0,1:T(8,128)(2,1)S(1)}, bf16[512,128]{0,1:T(8,128)(2,1)}, u32[]{:S(2)}) copy-start(bf16[512,128]{0,1:T(8,128)(2,1)} %copy-done.10) | copy-start | bytes 393220
  162.0 14.7 %collective-permute-start.17 = (bf16[512,128]{1,0:T(8,128)(2,1)}, bf16[512,128]{1,0:T(8,128)(2,1)S(1)}, u32[]{:S(2)}, u32[]{:S(2)}) collective-permute-start(bf16[512,128]{1,0:T(8,128)(2,1)} %copy.233), channel_id=1, source_target_pairs={{0,1},{1,2},{2,3},{3,4},{4,5},{5,6},{6,7},{8,9},{9,10},{10,11},{11... | collective-permute-start | bytes 393224 | tf_op jit(solution)/shard_map/ppermute | solution.py:53
  164.0 14.6 %collective-permute-start.16 = (bf16[512,128]{1,0:T(8,128)(2,1)}, bf16[512,128]{1,0:T(8,128)(2,1)S(1)}, u32[]{:S(2)}, u32[]{:S(2)}) collective-permute-start(bf16[512,128]{1,0:T(8,128)(2,1)} %copy.231), channel_id=1, source_target_pairs={{1,0},{2,1},{3,2},{4,3},{5,4},{6,5},{7,6},{9,8},{10,9},{11,10},{12... | collective-permute-start | bytes 393224 | tf_op jit(solution)/shard_map/ppermute | solution.py:53
  167.8 15.6 %collective-permute-start.15 = (bf16[512,128]{1,0:T(8,128)(2,1)}, bf16[512,128]{1,0:T(8,128)(2,1)S(1)}, u32[]{:S(2)}, u32[]{:S(2)}) collective-permute-start(bf16[512,128]{1,0:T(8,128)(2,1)} %copy.228), channel_id=1, source_target_pairs={{2,0},{3,1},{4,2},{5,3},{6,4},{7,5},{10,8},{11,9},{12,10},{13,11},... | collective-permute-start | bytes 393224 | tf_op jit(solution)/shard_map/ppermute | solution.py:53
  170.2 16.7 %collective-permute-start.18 = (bf16[512,128]{1,0:T(8,128)(2,1)}, bf16[512,128]{1,0:T(8,128)(2,1)S(1)}, u32[]{:S(2)}, u32[]{:S(2)}) collective-permute-start(bf16[512,128]{1,0:T(8,128)(2,1)} %copy.235), channel_id=1, source_target_pairs={{0,2},{1,3},{2,4},{3,5},{4,6},{5,7},{8,10},{9,11},{10,12},{11,13},... | collective-permute-start | bytes 393224 | tf_op jit(solution)/shard_map/ppermute | solution.py:53
  174.3 13.4 %collective-permute-start.19 = (bf16[512,128]{1,0:T(8,128)(2,1)}, bf16[512,128]{1,0:T(8,128)(2,1)S(1)}, u32[]{:S(2)}, u32[]{:S(2)}) collective-permute-start(bf16[512,128]{1,0:T(8,128)(2,1)} %copy.238), channel_id=1, source_target_pairs={{2,0},{3,1},{4,2},{5,3},{6,4},{7,5},{10,8},{11,9},{12,10},{13,11},... | collective-permute-start | bytes 393224 | tf_op jit(solution)/shard_map/ppermute | solution.py:53
  176.7 11.0 %collective-permute-start.20 = (bf16[512,128]{1,0:T(8,128)(2,1)}, bf16[512,128]{1,0:T(8,128)(2,1)S(1)}, u32[]{:S(2)}, u32[]{:S(2)}) collective-permute-start(bf16[512,128]{1,0:T(8,128)(2,1)} %copy.241), channel_id=1, source_target_pairs={{1,0},{2,1},{3,2},{4,3},{5,4},{6,5},{7,6},{9,8},{10,9},{11,10},{12... | collective-permute-start | bytes 393224 | tf_op jit(solution)/shard_map/ppermute | solution.py:53
  178.6 9.1 %collective-permute-start.21 = (bf16[512,128]{1,0:T(8,128)(2,1)}, bf16[512,128]{1,0:T(8,128)(2,1)S(1)}, u32[]{:S(2)}, u32[]{:S(2)}) collective-permute-start(bf16[512,128]{1,0:T(8,128)(2,1)} %copy.243), channel_id=1, source_target_pairs={{0,1},{1,2},{2,3},{3,4},{4,5},{5,6},{6,7},{8,9},{9,10},{10,11},{11... | collective-permute-start | bytes 393224 | tf_op jit(solution)/shard_map/ppermute | solution.py:53
  183.5 7.1 %collective-permute-start.22 = (bf16[512,128]{1,0:T(8,128)(2,1)}, bf16[512,128]{1,0:T(8,128)(2,1)S(1)}, u32[]{:S(2)}, u32[]{:S(2)}) collective-permute-start(bf16[512,128]{1,0:T(8,128)(2,1)} %copy.245), channel_id=1, source_target_pairs={{0,2},{1,3},{2,4},{3,5},{4,6},{5,7},{8,10},{9,11},{10,12},{11,13},... | collective-permute-start | bytes 393224 | tf_op jit(solution)/shard_map/ppermute | solution.py:53
Sparse Core Ops, SparseCore 0:
  88.0 16.0 all-gather.1
